TPU v7x, 32 devices: a whole 2x2x4 slice. The times are simulated.
32 devices in a mesh: dp: 8 (over y, x, core), mp: 4 (over z).
Axes of the slice: x: 2, y: 2, z: 4, core: 2. Of those that a mesh axis runs over, the one named last changes fastest.
Arguments:
- tokens: bfloat16 [16384, 768], P(('dp', 'mp')), may hold values from -6 to 6
- segment_ids: int32 [32, 512], P('dp'), may hold values from 0 to 7, never falling along the last dimension, each value on 1 to 128 neighbouring positions
- query_weight: bfloat16 [768, 768], P(None, 'mp'), may hold values from -0.21875 to 0.21875
- query_bias: bfloat16 [768], P('mp'), may hold values from -3 to 3
- key_weight: bfloat16 [768, 768], P(None, 'mp'), may hold values from -0.21875 to 0.21875
- value_weight: bfloat16 [768, 768], P(None, 'mp'), may hold values from -0.21875 to 0.21875
- value_bias: bfloat16 [768], P('mp'), may hold values from -3 to 3
- output_weight: bfloat16 [768, 768], P('mp'), may hold values from -0.875 to 0.875
- output_bias: bfloat16 [768], replicated, may hold values from -3 to 3
- first_gain: bfloat16 [768], replicated, may hold values from 0.25 to 1.75
- first_shift: bfloat16 [768], replicated, may hold values from -3 to 3
- up_weight: bfloat16 [768, 3072], P(None, 'mp'), may hold values from -0.21875 to 0.21875
- up_bias: bfloat16 [3072], P('mp'), may hold values from -3 to 3
- down_weight: bfloat16 [3072, 768], P('mp'), may hold values from -0.21875 to 0.21875
- down_bias: bfloat16 [768], replicated, may hold values from -3 to 3
- second_gain: bfloat16 [768], replicated, may hold values from 0.25 to 1.75
- second_shift: bfloat16 [768], replicated, may hold values from -3 to 3
- cotangent: bfloat16 [16384, 768], P(('dp', 'mp')), may hold values from -6 to 6
Outputs:
- output: bfloat16 [16384, 768], P(('dp', 'mp'))
- input_grad: bfloat16 [16384, 768], P(('dp', 'mp'))
- query_weight_grad: float32 [768, 768], P(None, 'mp')
- query_bias_grad: float32 [768], P('mp')
- key_weight_grad: float32 [768, 768], P(None, 'mp')
- value_weight_grad: float32 [768, 768], P(None, 'mp')
- value_bias_grad: float32 [768], P('mp')
- output_weight_grad: float32 [768, 768], P('mp')
- output_bias_grad: float32 [768], replicated
- first_gain_grad: float32 [768], replicated
- first_shift_grad: float32 [768], replicated
- up_weight_grad: float32 [768, 3072], P(None, 'mp')
- up_bias_grad: float32 [3072], P('mp')
- down_weight_grad: float32 [3072, 768], P('mp')
- down_bias_grad: float32 [768], replicated
- second_gain_grad: float32 [768], replicated
- second_shift_grad: float32 [768], replicated
Inputs may be any that keep to these rules, and one draw needn't show every extreme that they name: `segment_ids`: along each row of 512 tokens the ids never fall; each passage holds 1 to 128 tokens, and some passage holds exactly 128.
All inputs are finite; a program needn't handle non-finite values.
Results may differ from a plain program's by a relative error of at most 0.023.
Values may be sent and summed in bfloat16 or wider, within the bound.
No kernel may reach another device: no remote copies, remote signals or barrier semaphores. Data moves between devices by JAX's collectives and lax.ppermute only.
A program may use at most 128 MiB of HBM per device.

v0:
```python
import math
import jax
import jax.numpy as jnp
from jax import lax
from jax.sharding import PartitionSpec as P

HEAD_DIM = 64
GROUP = 8
epsilon = 1e-05
bf16 = jnp.bfloat16
f32 = jnp.float32


def inner_rows(left, right):
    return lax.dot_general(left, right, (((0,), (0,)), ((), ())), preferred_element_type=f32)


def norm_forward(total, norm_gain, norm_shift):
    average = jnp.mean(total, axis=-1, keepdims=True)
    centred = total - average
    inverse = lax.rsqrt(jnp.mean(centred * centred, axis=-1, keepdims=True) + epsilon)
    normal = centred * inverse
    return (normal * norm_gain + norm_shift, normal, inverse)


def norm_backward(grad_out, normal, inverse, norm_gain):
    scaled = grad_out * norm_gain
    return inverse * (
        scaled
        - jnp.mean(scaled, axis=-1, keepdims=True)
        - normal * jnp.mean(scaled * normal, axis=-1, keepdims=True)
    )


def gelu_slope(hidden):
    cumulative = 0.5 * (1.0 + lax.erf(hidden * 0.7071067811865476))
    density = jnp.exp(-0.5 * hidden * hidden) * 0.3989422804014327
    return cumulative + hidden * density


def masked_scores(queries, key_vecs, segment_row):
    scale_factor = 1.0 / math.sqrt(queries.shape[-1])
    scores = (
        jnp.einsum("qhd,khd->hqk", queries, key_vecs, preferred_element_type=f32) * scale_factor
    )
    allowed = segment_row[:, None] == segment_row[None, :]
    return jnp.where(allowed[None], scores, -1e30)


def row_forward(queries, key_vecs, values, segment_row):
    masked = masked_scores(queries, key_vecs, segment_row)
    highest_score = jnp.max(masked, axis=-1, keepdims=True)
    expo = jnp.exp(masked - highest_score)
    denominator = jnp.sum(expo, axis=-1, keepdims=True)
    probs = (expo / denominator).astype(bf16)
    context = jnp.einsum("hqk,khd->qhd", probs, values, preferred_element_type=f32)
    log_total = highest_score[..., 0] + jnp.log(denominator[..., 0])
    return (context.astype(bf16), log_total)


def row_backward(queries, key_vecs, values, segment_row, log_total, grad_context):
    scale_factor = 1.0 / math.sqrt(queries.shape[-1])
    masked = masked_scores(queries, key_vecs, segment_row)
    probs = jnp.exp(masked - log_total[..., None])
    grad_probs = jnp.einsum("qhd,khd->hqk", grad_context, values, preferred_element_type=f32)
    grad_values = jnp.einsum(
        "hqk,qhd->khd", probs.astype(bf16), grad_context, preferred_element_type=f32
    )
    inner = jnp.sum(grad_probs * probs, axis=-1, keepdims=True)
    grad_scores = (probs * (grad_probs - inner)).astype(bf16)
    grad_queries = (
        jnp.einsum("hqk,khd->qhd", grad_scores, key_vecs, preferred_element_type=f32) * scale_factor
    )
    grad_keys = (
        jnp.einsum("hqk,qhd->khd", grad_scores, queries, preferred_element_type=f32) * scale_factor
    )
    return (grad_queries.astype(bf16), grad_keys.astype(bf16), grad_values.astype(bf16))


def solution(mesh):
    n_dp, n_mp = (mesh.shape["dp"], mesh.shape["mp"])
    if n_dp % GROUP:
        raise ValueError("dp size")

    def rotate(array, step):
        return lax.ppermute(array, "mp", [(i, (i + step) % n_mp) for i in range(n_mp)])

    def swap(array, bits):
        return lax.ppermute(array, "dp", [(i, i ^ bits) for i in range(n_dp)])

    def plane_gather(array):
        four = jnp.stack([array, swap(array, 2), swap(array, 4), swap(array, 6)])
        other = swap(four, 1)
        return jnp.stack([four, other], axis=1).reshape((GROUP,) + array.shape)

    def gather_weights(quarter, order, extra=None):
        rows = quarter.shape[0] // GROUP
        index = lax.axis_index("dp") % GROUP
        piece = lax.dynamic_slice_in_dim(quarter, index * rows, rows, 0)
        if extra is not None:
            piece = jnp.concatenate([piece, extra])
        got = [rotate(piece, r) for r in range(1, n_mp)]
        slots = plane_gather(jnp.stack([g[:rows] for g in got]))
        slots = slots[order].transpose(1, 0, 2, 3).reshape((n_mp - 1,) + quarter.shape)
        full = jnp.concatenate([quarter[None], slots])
        if extra is None:
            return full
        return (full, jnp.stack([extra] + [g[rows:] for g in got]))

    def reduce_grads(grads, order):
        quarters, height, width = grads.shape
        rows = height // GROUP
        half = width // 2
        slots = grads.astype(bf16).reshape(quarters, GROUP, rows, width)[:, order]
        slots = slots.reshape(quarters, GROUP // 2, 2, rows, width)
        part = (slots[:, :, 0].astype(f32) + swap(slots[:, :, 1], 1).astype(f32)).astype(bf16)
        left, right = (part[..., :half], part[..., half:])
        left_got = swap(left[:, jnp.array([1, 3])], 2)
        right_got = swap(right[:, 2:], 4)
        left = (left[:, jnp.array([0, 2])].astype(f32) + left_got.astype(f32)).astype(bf16)
        right = (right[:, :2].astype(f32) + right_got.astype(f32)).astype(bf16)
        left_got = swap(left[:, 1], 4)
        right_got = swap(right[:, 1], 2)
        left = left[:, 0].astype(f32) + left_got.astype(f32)
        right = right[:, 0].astype(f32) + right_got.astype(f32)
        part = jnp.concatenate([left, right], axis=-1).astype(bf16)
        total = part[0].astype(f32)
        for r in range(1, n_mp):
            total = total + rotate(part[r], -r).astype(f32)
        if n_dp > GROUP:
            total = lax.psum(
                total,
                "dp",
                axis_index_groups=[
                    [i + GROUP * k for k in range(n_dp // GROUP)] for i in range(GROUP)
                ],
            )
        return plane_gather(total.astype(bf16))[order].astype(f32).reshape(height, width)

    def shards(
        tokens,
        segment_ids,
        query_weight,
        query_bias,
        key_weight,
        value_weight,
        value_bias,
        output_weight,
        output_bias,
        first_gain,
        first_shift,
        up_weight,
        up_bias,
        down_weight,
        down_bias,
        second_gain,
        second_shift,
        cotangent,
    ):
        length, width = tokens.shape
        head_width = query_weight.shape[1]
        units = up_weight.shape[1]
        heads = n_mp * head_width // HEAD_DIM
        order = jnp.arange(GROUP) ^ lax.axis_index("dp") % GROUP
        place = lax.axis_index("mp")
        row = lax.dynamic_index_in_dim(segment_ids, place, 0, keepdims=False)
        biases = jnp.zeros((8, units), bf16)
        biases = biases.at[0, :head_width].set(query_bias)
        biases = biases.at[0, head_width : 2 * head_width].set(value_bias)
        biases = biases.at[1].set(up_bias)
        att_quarter = jnp.concatenate(
            [query_weight, key_weight, value_weight, output_weight.T], axis=1
        )
        att, biases = gather_weights(att_quarter, order, biases)
        up = gather_weights(up_weight, order)
        down = gather_weights(down_weight, order)

        def columns(array):
            return array.transpose(1, 0, 2).reshape(array.shape[1], -1)

        w = head_width
        query_all, key_all, value_all, output_all = (
            columns(att[:, :, i * w : (i + 1) * w]) for i in range(4)
        )
        up_all, down_all = (columns(up), down.reshape(-1, width))
        query_bias_all = biases[:, 0, :w].reshape(-1)
        value_bias_all = biases[:, 0, w : 2 * w].reshape(-1)
        up_bias_all = biases[:, 1].reshape(-1)

        def by_heads(array):
            return array.reshape(length, heads, HEAD_DIM)

        def flat(array):
            return array.reshape(length, heads * HEAD_DIM)

        def mm(left, right):
            return jnp.dot(left, right, preferred_element_type=f32)

        def mmt(left, right):
            return lax.dot_general(
                left, right, (((1,), (1,)), ((), ())), preferred_element_type=f32
            )

        queries = by_heads((mm(tokens, query_all) + query_bias_all).astype(bf16))
        key_vecs = by_heads(mm(tokens, key_all).astype(bf16))
        values = by_heads((mm(tokens, value_all) + value_bias_all).astype(bf16))
        contexts, log_total = row_forward(queries, key_vecs, values, row)
        contexts = flat(contexts)
        attended = mmt(contexts, output_all) + output_bias
        gain_one = first_gain.astype(f32)
        gain_two = second_gain.astype(f32)
        normed_one, normal_one, inverse_one = norm_forward(
            tokens.astype(f32) + attended, gain_one, first_shift.astype(f32)
        )
        normed_low = normed_one.astype(bf16)
        hidden = mm(normed_low, up_all) + up_bias_all
        activated = jax.nn.gelu(hidden, approximate=False).astype(bf16)
        mixed = mm(activated, down_all) + down_bias
        result, normal_two, inverse_two = norm_forward(
            normed_one + mixed, gain_two, second_shift.astype(f32)
        )
        grad_out = cotangent.astype(f32)
        grad_second_gain = jnp.sum(grad_out * normal_two, axis=0)
        grad_second_shift = jnp.sum(grad_out, axis=0)
        grad_two = norm_backward(grad_out, normal_two, inverse_two, gain_two)
        grad_mixed = grad_two.astype(bf16)
        grad_down_bias = jnp.sum(grad_mixed.astype(f32), axis=0)
        grad_down = inner_rows(activated, grad_mixed).reshape(n_mp, units, width)
        grad_down = reduce_grads(grad_down, order)
        grad_hidden = (mmt(grad_mixed, down_all) * gelu_slope(hidden)).astype(bf16)
        grad_up_bias = jnp.sum(grad_hidden.astype(f32), axis=0)

        def quarters(array):
            return array.reshape(array.shape[0], n_mp, -1).transpose(1, 0, 2)

        grad_up = reduce_grads(quarters(inner_rows(normed_low, grad_hidden)), order)
        grad_normed = mmt(grad_hidden, up_all) + grad_two
        grad_first_gain = jnp.sum(grad_normed * normal_one, axis=0)
        grad_first_shift = jnp.sum(grad_normed, axis=0)
        grad_one = norm_backward(grad_normed, normal_one, inverse_one, gain_one)
        grad_attended = grad_one.astype(bf16)
        grad_output_bias = jnp.sum(grad_attended.astype(f32), axis=0)
        grad_contexts = mm(grad_attended, output_all).astype(bf16)
        grad_queries, grad_keys, grad_values = map(
            flat, row_backward(queries, key_vecs, values, row, log_total, by_heads(grad_contexts))
        )
        grad_query_bias = jnp.sum(grad_queries.astype(f32), axis=0)
        grad_value_bias = jnp.sum(grad_values.astype(f32), axis=0)
        grad_att = jnp.concatenate(
            [
                quarters(inner_rows(tokens, grad_queries)),
                quarters(inner_rows(tokens, grad_keys)),
                quarters(inner_rows(tokens, grad_values)),
                quarters(inner_rows(grad_attended, contexts)),
            ],
            axis=-1,
        )
        grad_att = reduce_grads(grad_att, order)
        grad_tokens = (
            mmt(grad_queries, query_all)
            + mmt(grad_keys, key_all)
            + mmt(grad_values, value_all)
            + grad_one
        )
        mine = jnp.concatenate(
            [
                grad_query_bias.reshape(n_mp, -1),
                grad_value_bias.reshape(n_mp, -1),
                grad_up_bias.reshape(n_mp, -1),
            ],
            axis=1,
        )
        mine = mine[(place - jnp.arange(n_mp)) % n_mp]
        shared = jnp.stack(
            [
                grad_output_bias,
                grad_first_gain,
                grad_first_shift,
                grad_down_bias,
                grad_second_gain,
                grad_second_shift,
            ]
        )
        mine, shared = lax.psum((mine, shared), ("dp", "mp"))
        mine = lax.dynamic_index_in_dim(mine, place, 0, keepdims=False)
        return (
            result.astype(bf16),
            grad_tokens.astype(bf16),
            grad_att[:, :w],
            mine[:w],
            grad_att[:, w : 2 * w],
            grad_att[:, 2 * w : 3 * w],
            mine[w : 2 * w],
            grad_att[:, 3 * w :].T,
            shared[0],
            shared[1],
            shared[2],
            grad_up,
            mine[2 * w :],
            grad_down,
            shared[3],
            shared[4],
            shared[5],
        )

    in_specs = (
        P(("dp", "mp"), None),
        P("dp", None),
        P(None, "mp"),
        P("mp"),
        P(None, "mp"),
        P(None, "mp"),
        P("mp"),
        P("mp", None),
        P(),
        P(),
        P(),
        P(None, "mp"),
        P("mp"),
        P("mp", None),
        P(),
        P(),
        P(),
        P(("dp", "mp"), None),
    )
    out_specs = (
        P(("dp", "mp"), None),
        P(("dp", "mp"), None),
        P(None, "mp"),
        P("mp"),
        P(None, "mp"),
        P(None, "mp"),
        P("mp"),
        P("mp", None),
        P(),
        P(),
        P(),
        P(None, "mp"),
        P("mp"),
        P("mp", None),
        P(),
        P(),
        P(),
    )
    return jax.shard_map(shards, mesh=mesh, in_specs=in_specs, out_specs=out_specs, check_vma=False)
```

profile of v0, /device:TPU:1, one launch (start us, length us, event | category | flops | bytes accessed | tf_op | source)
XLA Modules:
  0.0 501.2 jit_solution(7196510737156142588)
XLA Ops:
  1.7 4.2 collective-permute-start.16
  7.3 2.9 collective-permute-start.9
  21.3 3.2 collective-permute-start.2
  28.9 2.5 collective-permute-done.8
  35.7 8.9 %collective-permute-done.1 = bf16[104,768]{1,0:T(8,128)(2,1)S(1)} collective-permute-done((bf16[104,768]{1,0:T(8,128)(2,1)S(1)}, bf16[104,768]{1,0:T(8,128)(2,1)S(1)}, u32[]{:S(2)}, u32[]{:S(2)}) %collective-permute-start.1) | collective-permute-done | bytes 159776 | tf_op jit(solution)/shard_map/ppermute | solution.py:86
  47.3 3.4 collective-permute-done.19
  52.7 10.4 %collective-permute-start.20 = (bf16[4,3,96,768]{3,2,1,0:T(8,128)(2,1)}, bf16[4,3,96,768]{3,2,1,0:T(8,128)(2,1)S(1)}, u32[]{:S(2)}, u32[]{:S(2)}) collective-permute-start(bf16[4,3,96,768]{3,2,1,0:T(8,128)(2,1)} %get-tuple-element.135), channel_id=1, source_target_pairs={{0,4},{4,0},{8,12},{12,8},{16,20},{20,16},{24,28},{28,24},{1,5},{5... | collective-permute-start | bytes 5308424 | tf_op jit(solution)/shard_map/ppermute | solution.py:89
  64.5 5.1 %collective-permute-done.12 = bf16[3,96,768]{2,1,0:T(8,128)(2,1)S(1)} collective-permute-done((bf16[3,96,768]{2,1,0:T(8,128)(2,1)S(1)}, bf16[3,96,768]{2,1,0:T(8,128)(2,1)S(1)}, u32[]{:S(2)}, u32[]{:S(2)}) %collective-permute-start.12) | collective-permute-done | bytes 442400 | tf_op jit(solution)/shard_map/ppermute | solution.py:89
  71.7 5.5 %collective-permute-start.13 = (bf16[4,3,96,768]{3,2,1,0:T(8,128)(2,1)}, bf16[4,3,96,768]{3,2,1,0:T(8,128)(2,1)}, u32[]{:S(2)}, u32[]{:S(2)}) collective-permute-start(bf16[4,3,96,768]{3,2,1,0:T(8,128)(2,1)} %get-tuple-element.139), channel_id=1, source_target_pairs={{0,4},{4,0},{8,12},{12,8},{16,20},{20,16},{24,28},{28,24},{1,5},{5... | collective-permute-start | bytes 5308424 | tf_op jit(solution)/shard_map/ppermute | solution.py:89
  82.5 6.6 %collective-permute-done.4 = bf16[3,96,768]{2,1,0:T(8,128)(2,1)S(1)} collective-permute-done((bf16[3,96,768]{2,1,0:T(8,128)(2,1)S(1)}, bf16[3,96,768]{2,1,0:T(8,128)(2,1)S(1)}, u32[]{:S(2)}, u32[]{:S(2)}) %collective-permute-start.4) | collective-permute-done | bytes 442400 | tf_op jit(solution)/shard_map/ppermute | solution.py:89
  89.1 10.3 %collective-permute-done.5 = bf16[3,96,768]{2,1,0:T(8,128)(2,1)S(1)} collective-permute-done((bf16[3,96,768]{2,1,0:T(8,128)(2,1)S(1)}, bf16[3,96,768]{2,1,0:T(8,128)(2,1)S(1)}, u32[]{:S(2)}, u32[]{:S(2)}) %collective-permute-start.5) | collective-permute-done | bytes 442400 | tf_op jit(solution)/shard_map/ppermute | solution.py:89
  109.5 2.5 gather_fusion.2
  112.0 4.2 copy.146
  118.0 2.5 gather_fusion.1
  122.9 2.6 maximum_bitcast_fusion
  125.5 7.4 %copy.144 = bf16[768,4,768]{0,2,1:T(8,128)(2,1)} copy(bf16[768,4,768]{2,0,1:T(8,128)(2,1)} %maximum_bitcast_fusion) | data formatting | bytes 9437184 | tf_op jit(solution)/shard_map/transpose | solution.py:179
  132.9 4.0 pad_maximum_fusion
  139.0 2.5 gather_fusion
  143.8 2.9 fusion.39
  146.8 2.5 copy.141
  149.3 2.5 copy.137
  160.0 2.6 fusion
  165.6 3.8 fusion.44
  170.8 15.7 %fusion.4 = (bf16[512,3072]{1,0:T(8,128)(2,1)S(1)}, f32[512,3072]{1,0:T(8,128)S(1)}) fusion(f32[3072]{0:T(1024)S(1)} %bitcast.450, bf16[768,3072]{0,1:T(8,128)(2,1)S(1)} %bitcast.380, f32[512,768]{1,0:T(8,128)S(1)} %get-tuple-element.169, f32[768]{0:T(1024)S(1)} %copy-done.38, f32[768]{0:T(1024)S(1)} %convert_element_type.401, f32[512]{0:T(512)S(1)} %add_rsqrt_fusion.1, ...), kind=kOutput, calls=%fused_computation.31 | convolution fusion | flops 2521694208 | bytes 15751168 | tf_op jit(solution)/shard_map/dot_general | solution.py:197
  186.5 2.7 fusion.116
  192.0 4.6 convert_reduce_fusion
  196.6 3.0 multiply_reduce_fusion.1
  199.6 5.2 %convolution_convert_fusion.1 = bf16[768,3072]{1,0:T(8,128)(2,1)} fusion(bf16[512,3072]{1,0:T(8,128)(2,1)S(1)} %get-tuple-element.182, f32[512,768]{1,0:T(8,128)S(1)} %get-tuple-element.169, f32[768]{0:T(1024)S(1)} %copy-done.38, f32[768]{0:T(1024)S(1)} %convert_element_type.401, f32[512]{0:T(512)S(1)} %add_rsqrt_fusion.1, f32[512]{0:T(512)S(1)} %broadcast_multiply_fusion.5), kind=kOutput, calls=%fused_computation.58 | convolution fusion | flops 2420244480 | bytes 9447424 | tf_op jit(solution)/shard_map/dot_general | solution.py:15
  204.8 4.3 convolution_convert_fusion
  212.8 7.4 %convert_reduce_fusion.4 = (f32[12,64]{1,0:T(8,128)S(1)}, bf16[12,64,512]{2,1,0:T(8,128)(2,1)}) fusion(bf16[512,12,64]{0,2,1:T(8,128)(2,1)S(1)} %bitcast.391, f32[12,512]{1,0:T(8,128)S(1)} %log_add_fusion, f32[12,512,512]{1,2,0:T(8,128)} %copy-done.2, pred[512,512]{0,1:T(8,128)(4,1)S(1)} %copy-done.9), kind=kOutput, calls=%fused_computation.105 | convolution fusion | flops 416414976 | bytes 14445568 | tf_op jit(solution)/shard_map/hqk,qhd->khd/dot_general | solution.py:66
  220.2 9.6 %multiply_reduce_fusion = (f32[12,512]{1,0:T(8,128)S(1)}, f32[12,512,512]{1,2,0:T(8,128)}) fusion(f32[12,512]{1,0:T(8,128)S(1)} %log_add_fusion, f32[12,512,512]{1,2,0:T(8,128)} %copy-done.2, pred[512,512]{0,1:T(8,128)(4,1)S(1)} %copy-done.9, bf16[512,12,64]{0,2,1:T(8,128)(2,1)S(1)} %bitcast.392, bf16[512,12,64]{0,2,1:T(8,128)(2,1)S(1)} %bitcast.410), kind=kOutput, calls=%fused_computation.17 | convolution fusion | flops 418375680 | bytes 27049984 | tf_op jit(solution)/shard_map/qhd,khd->hqk/dot_general | solution.py:65
  229.9 6.8 %multiply_convert_fusion = bf16[12,512,512]{1,2,0:T(8,128)(2,1)S(1)} fusion(f32[12,512,512]{1,2,0:T(8,128)} %get-tuple-element.176, f32[12,512]{1,0:T(8,128)S(1)} %get-tuple-element.175, f32[12,512]{1,0:T(8,128)S(1)} %log_add_fusion, f32[12,512,512]{1,2,0:T(8,128)S(1)} %bitcast.347, pred[512,512]{0,1:T(8,128)(4,1)S(1)} %copy-done.9), kind=kLoop, calls=%fused_computation.16 | loop fusion | flops 18874368 | bytes 31768576 | tf_op jit(solution)/shard_map/convert_element_type | solution.py:70
  236.7 3.0 multiply_convert_fusion.1
  245.3 3.2 convolution_convert_fusion.3
  248.5 2.5 copy.153
  251.0 5.4 %gather_fusion.12 = bf16[8,4,96,768]{3,2,1,0:T(8,128)(2,1)} fusion(bf16[4,8,96,768]{3,2,1,0:T(8,128)(2,1)} %bitcast.386, s32[1024]{0:T(1024)S(1)} %copy-done.35), kind=kCustom, calls=%fused_computation.12 | custom fusion | bytes 9437216 | tf_op jit(solution)/shard_map/gather | solution.py:114
  256.4 2.7 copy.166
  262.9 2.5 copy.151
  265.4 3.2 convolution_convert_fusion.4
  268.6 2.5 copy.152
  271.1 6.6 %pad_maximum_fusion.1 = bf16[4,8,96,768]{3,2,1,0:T(8,128)(2,1)} fusion(bf16[4,8,96,192]{3,2,1,0:T(8,128)(2,1)S(1)} %bitcast.371, bf16[4,8,96,192]{3,2,1,0:T(8,128)(2,1)} %bitcast.372, bf16[4,8,96,192]{3,2,1,0:T(8,128)(2,1)} %bitcast.374, bf16[4,8,96,192]{3,2,1,0:T(8,128)(2,1)} %bitcast.373), kind=kLoop, calls=%fused_computation.64 | loop fusion | flops 18874368 | bytes 9437184 | tf_op jit(solution)/shard_map/concatenate | solution.py:249
  277.7 9.7 %convert_element_type.455 = bf16[768,4,768]{2,1,0:T(4,128)(2,1)} reshape(bf16[768,3072]{1,0:T(8,128)(2,1)} %convolution_convert_fusion.1) | data formatting | bytes 9437184 | tf_op jit(solution)/shard_map/convert_element_type | solution.py:114
  287.4 5.1 %copy.161 = bf16[4,768,768]{2,1,0:T(8,128)(2,1)} copy(bf16[4,768,768]{2,0,1:T(4,128)(2,1)} %bitcast.356) | data formatting | bytes 9437184 | tf_op jit(solution)/shard_map/convert_element_type | solution.py:114
  292.5 5.4 %gather_fusion.8 = bf16[8,4,96,768]{3,2,1,0:T(8,128)(2,1)} fusion(bf16[4,8,96,768]{3,2,1,0:T(8,128)(2,1)} %bitcast.357, s32[1024]{0:T(1024)S(1)} %copy-done.35), kind=kCustom, calls=%fused_computation.8 | custom fusion | bytes 9437216 | tf_op jit(solution)/shard_map/gather | solution.py:114
  297.9 4.8 copy.162
  302.7 5.4 %gather_fusion.3 = bf16[8,4,96,768]{3,2,1,0:T(8,128)(2,1)} fusion(bf16[4,8,96,768]{3,2,1,0:T(8,128)(2,1)} %pad_maximum_fusion.1, s32[1024]{0:T(1024)S(1)} %copy-done.35), kind=kCustom, calls=%fused_computation.3 | custom fusion | bytes 9437216 | tf_op jit(solution)/shard_map/gather | solution.py:114
  308.1 3.4 slice_bitcast_fusion.2
  315.1 44.2 %all-reduce.1 = (f32[4,1152]{1,0:T(4,128)}, f32[6,768]{1,0:T(8,128)}) all-reduce(f32[4,1152]{1,0:T(4,128)S(1)} %gather_fusion.7, f32[6,768]{1,0:T(8,128)S(1)} %stack.271), channel_id=1, replica_groups=mesh['dp'=8,'mp'=4] {'dp','mp'}, use_global_device_ids=true, to_apply=%region_15.16 | all-reduce | flops 9216 | bytes 73728 | tf_op jit(solution)/shard_map/psum | solution.py:284
  364.9 2.5 fusion.22
  373.0 3.1 fusion.24
  376.0 3.1 fusion.23
  383.3 2.8 gather_fusion.10
  386.1 2.7 gather_fusion.9
  400.0 5.2 %collective-permute-done.36 = bf16[4,2,96,384]{3,2,1,0:T(8,128)(2,1)S(1)} collective-permute-done((bf16[4,2,96,384]{3,2,1,0:T(8,128)(2,1)}, bf16[4,2,96,384]{3,2,1,0:T(8,128)(2,1)S(1)}, u32[]{:S(2)}, u32[]{:S(2)}) %collective-permute-start.36) | collective-permute-done | bytes 589856 | tf_op jit(solution)/shard_map/ppermute | solution.py:89
  409.1 8.7 %collective-permute-done.24 = bf16[4,2,96,384]{3,2,0,1:T(8,128)(2,1)S(1)} collective-permute-done((bf16[4,2,96,384]{3,2,0,1:T(8,128)(2,1)}, bf16[4,2,96,384]{3,2,0,1:T(8,128)(2,1)S(1)}, u32[]{:S(2)}, u32[]{:S(2)}) %collective-permute-start.24) | collective-permute-done | bytes 589856 | tf_op jit(solution)/shard_map/ppermute | solution.py:89
  420.7 5.3 %collective-permute-done.49 = bf16[4,96,384]{2,1,0:T(8,128)(2,1)S(1)} collective-permute-done((bf16[4,96,384]{2,1,0:T(8,128)(2,1)S(1)}, bf16[4,96,384]{2,1,0:T(8,128)(2,1)S(1)}, u32[]{:S(2)}, u32[]{:S(2)}) %collective-permute-start.49) | collective-permute-done | bytes 294944 | tf_op jit(solution)/shard_map/ppermute | solution.py:89
  428.2 4.1 collective-permute-done.37
  434.8 3.8 collective-permute-done.25
  442.4 2.8 collective-permute-done.38
  445.2 3.0 collective-permute-done.40
  448.5 9.1 %collective-permute-done.39 = bf16[96,768]{1,0:T(8,128)(2,1)S(1)} collective-permute-done((bf16[96,768]{1,0:T(8,128)(2,1)S(1)}, bf16[96,768]{1,0:T(8,128)(2,1)S(1)}, u32[]{:S(2)}, u32[]{:S(2)}) %collective-permute-start.39) | collective-permute-done | bytes 147488 | tf_op jit(solution)/shard_map/ppermute | solution.py:86
  464.4 3.5 collective-permute-done.42
  467.9 2.6 collective-permute-start.56
  480.0 7.9 %collective-permute-start.32 = (bf16[4,96,768]{2,1,0:T(8,128)(2,1)}, bf16[4,96,768]{2,1,0:T(8,128)(2,1)}, u32[]{:S(2)}, u32[]{:S(2)}) collective-permute-start(bf16[4,96,768]{2,1,0:T(8,128)(2,1)} %get-tuple-element.152), channel_id=1, source_target_pairs={{0,4},{4,0},{8,12},{12,8},{16,20},{20,16},{24,28},{28,24},{1,5},{5... | collective-permute-start | bytes 1769480 | tf_op jit(solution)/shard_map/ppermute | solution.py:89
  (379 shorter events, 157.0 us)
Async XLA Ops:
  0.7 25.3 %copy-start = (s32[4,512]{1,0:T(4,128)S(1)}, s32[4,512]{1,0:T(4,128)}, u32[]{:S(2)}) copy-start(s32[4,512]{1,0:T(4,128)} %param.31) | copy-start | bytes 24580
  1.7 19.6 %collective-permute-start.16 = (bf16[96,768]{1,0:T(8,128)(2,1)S(1)}, bf16[96,768]{1,0:T(8,128)(2,1)S(1)}, u32[]{:S(2)}, u32[]{:S(2)}) collective-permute-start(bf16[96,768]{1,0:T(8,128)(2,1)S(1)} %constant_dynamic-slice_fusion.1), channel_id=1, source_target_pairs={{0,3},{1,0},{2,1},{3,2},{4,7},{5,4},{6,5},{7,6},{8,11},{9,8},{10,9... | collective-permute-start | bytes 442376 | tf_op jit(solution)/shard_map/ppermute | solution.py:86
  5.9 15.4 %collective-permute-start.15 = (bf16[96,768]{1,0:T(8,128)(2,1)S(1)}, bf16[96,768]{1,0:T(8,128)(2,1)S(1)}, u32[]{:S(2)}, u32[]{:S(2)}) collective-permute-start(bf16[96,768]{1,0:T(8,128)(2,1)S(1)} %constant_dynamic-slice_fusion.1), channel_id=1, source_target_pairs={{0,2},{1,3},{2,0},{3,1},{4,6},{5,7},{6,4},{7,5},{8,10},{9,11},{10,... | collective-permute-start | bytes 442376 | tf_op jit(solution)/shard_map/ppermute | solution.py:86
  5.9 18.7 %collective-permute-start.14 = (bf16[96,768]{1,0:T(8,128)(2,1)S(1)}, bf16[96,768]{1,0:T(8,128)(2,1)S(1)}, u32[]{:S(2)}, u32[]{:S(2)}) collective-permute-start(bf16[96,768]{1,0:T(8,128)(2,1)S(1)} %constant_dynamic-slice_fusion.1), channel_id=1, source_target_pairs={{0,1},{1,2},{2,3},{3,0},{4,5},{5,6},{6,7},{7,4},{8,9},{9,10},{10,1... | collective-permute-start | bytes 442376 | tf_op jit(solution)/shard_map/ppermute | solution.py:86
  7.3 19.3 %collective-permute-start.9 = (bf16[96,768]{1,0:T(8,128)(2,1)S(1)}, bf16[96,768]{1,0:T(8,128)(2,1)S(1)}, u32[]{:S(2)}, u32[]{:S(2)}) collective-permute-start(bf16[96,768]{1,0:T(8,128)(2,1)S(1)} %constant_dynamic-slice_fusion.2), channel_id=1, source_target_pairs={{0,3},{1,0},{2,1},{3,2},{4,7},{5,4},{6,5},{7,6},{8,11},{9,8},{10,9... | collective-permute-start | bytes 442376 | tf_op jit(solution)/shard_map/ppermute | solution.py:86
  10.1 21.2 %collective-permute-start.8 = (bf16[96,768]{1,0:T(8,128)(2,1)S(1)}, bf16[96,768]{1,0:T(8,128)(2,1)S(1)}, u32[]{:S(2)}, u32[]{:S(2)}) collective-permute-start(bf16[96,768]{1,0:T(8,128)(2,1)S(1)} %constant_dynamic-slice_fusion.2), channel_id=1, source_target_pairs={{0,2},{1,3},{2,0},{3,1},{4,6},{5,7},{6,4},{7,5},{8,10},{9,11},{10,... | collective-permute-start | bytes 442376 | tf_op jit(solution)/shard_map/ppermute | solution.py:86
  21.3 11.9 %collective-permute-start.7 = (bf16[96,768]{1,0:T(8,128)(2,1)S(1)}, bf16[96,768]{1,0:T(8,128)(2,1)S(1)}, u32[]{:S(2)}, u32[]{:S(2)}) collective-permute-start(bf16[96,768]{1,0:T(8,128)(2,1)S(1)} %constant_dynamic-slice_fusion.2), channel_id=1, source_target_pairs={{0,1},{1,2},{2,3},{3,0},{4,5},{5,6},{6,7},{7,4},{8,9},{9,10},{10,1... | collective-permute-start | bytes 442376 | tf_op jit(solution)/shard_map/ppermute | solution.py:86
  21.3 13.1 %collective-permute-start.2 = (bf16[104,768]{1,0:T(8,128)(2,1)S(1)}, bf16[104,768]{1,0:T(8,128)(2,1)S(1)}, u32[]{:S(2)}, u32[]{:S(2)}) collective-permute-start(bf16[104,768]{1,0:T(8,128)(2,1)S(1)} %pad_maximum_fusion.19), channel_id=1, source_target_pairs={{0,3},{1,0},{2,1},{3,2},{4,7},{5,4},{6,5},{7,6},{8,11},{9,8},{10,9... | collective-permute-start | bytes 479240 | tf_op jit(solution)/shard_map/ppermute | solution.py:86
  24.6 22.4 %collective-permute-start.18 = (bf16[3,96,768]{2,1,0:T(8,128)(2,1)S(1)}, bf16[3,96,768]{2,1,0:T(8,128)(2,1)S(1)}, u32[]{:S(2)}, u32[]{:S(2)}) collective-permute-start(bf16[3,96,768]{2,1,0:T(8,128)(2,1)S(1)} %get-tuple-element.157), channel_id=1, source_target_pairs={{0,16},{4,20},{8,24},{12,28},{16,0},{20,4},{24,8},{28,12},{1,17},{... | collective-permute-start | bytes 1327112 | tf_op jit(solution)/shard_map/ppermute | solution.py:89
  26.6 18.0 %collective-permute-start.1 = (bf16[104,768]{1,0:T(8,128)(2,1)S(1)}, bf16[104,768]{1,0:T(8,128)(2,1)S(1)}, u32[]{:S(2)}, u32[]{:S(2)}) collective-permute-start(bf16[104,768]{1,0:T(8,128)(2,1)S(1)} %pad_maximum_fusion.19), channel_id=1, source_target_pairs={{0,2},{1,3},{2,0},{3,1},{4,6},{5,7},{6,4},{7,5},{8,10},{9,11},{10,... | collective-permute-start | bytes 479240 | tf_op jit(solution)/shard_map/ppermute | solution.py:86
  31.3 14.5 %collective-permute-start = (bf16[104,768]{1,0:T(8,128)(2,1)S(1)}, bf16[104,768]{1,0:T(8,128)(2,1)S(1)}, u32[]{:S(2)}, u32[]{:S(2)}) collective-permute-start(bf16[104,768]{1,0:T(8,128)(2,1)S(1)} %pad_maximum_fusion.19), channel_id=1, source_target_pairs={{0,1},{1,2},{2,3},{3,0},{4,5},{5,6},{6,7},{7,4},{8,9},{9,10},{10,1... | collective-permute-start | bytes 479240 | tf_op jit(solution)/shard_map/ppermute | solution.py:86
  33.1 14.2 %collective-permute-start.17 = (bf16[3,96,768]{2,1,0:T(8,128)(2,1)S(1)}, bf16[3,96,768]{2,1,0:T(8,128)(2,1)S(1)}, u32[]{:S(2)}, u32[]{:S(2)}) collective-permute-start(bf16[3,96,768]{2,1,0:T(8,128)(2,1)S(1)} %get-tuple-element.157), channel_id=1, source_target_pairs={{0,8},{4,12},{8,0},{12,4},{16,24},{20,28},{24,16},{28,20},{1,9},{5... | collective-permute-start | bytes 1327112 | tf_op jit(solution)/shard_map/ppermute | solution.py:89
  34.4 16.2 %collective-permute-start.19 = (bf16[3,96,768]{2,1,0:T(8,128)(2,1)S(1)}, bf16[3,96,768]{2,1,0:T(8,128)(2,1)S(1)}, u32[]{:S(2)}, u32[]{:S(2)}) collective-permute-start(bf16[3,96,768]{2,1,0:T(8,128)(2,1)S(1)} %get-tuple-element.157), channel_id=1, source_target_pairs={{0,24},{4,28},{8,16},{12,20},{16,8},{20,12},{24,0},{28,4},{1,25},{... | collective-permute-start | bytes 1327112 | tf_op jit(solution)/shard_map/ppermute | solution.py:89
  44.6 20.0 %collective-permute-start.11 = (bf16[3,96,768]{2,1,0:T(8,128)(2,1)S(1)}, bf16[3,96,768]{2,1,0:T(8,128)(2,1)S(1)}, u32[]{:S(2)}, u32[]{:S(2)}) collective-permute-start(bf16[3,96,768]{2,1,0:T(8,128)(2,1)S(1)} %get-tuple-element.161), channel_id=1, source_target_pairs={{0,16},{4,20},{8,24},{12,28},{16,0},{20,4},{24,8},{28,12},{1,17},{... | collective-permute-start | bytes 1327112 | tf_op jit(solution)/shard_map/ppermute | solution.py:89
  45.8 18.7 %collective-permute-start.10 = (bf16[3,96,768]{2,1,0:T(8,128)(2,1)S(1)}, bf16[3,96,768]{2,1,0:T(8,128)(2,1)S(1)}, u32[]{:S(2)}, u32[]{:S(2)}) collective-permute-start(bf16[3,96,768]{2,1,0:T(8,128)(2,1)S(1)} %get-tuple-element.161), channel_id=1, source_target_pairs={{0,8},{4,12},{8,0},{12,4},{16,24},{20,28},{24,16},{28,20},{1,9},{5... | collective-permute-start | bytes 1327112 | tf_op jit(solution)/shard_map/ppermute | solution.py:89
  47.0 22.6 %collective-permute-start.12 = (bf16[3,96,768]{2,1,0:T(8,128)(2,1)S(1)}, bf16[3,96,768]{2,1,0:T(8,128)(2,1)S(1)}, u32[]{:S(2)}, u32[]{:S(2)}) collective-permute-start(bf16[3,96,768]{2,1,0:T(8,128)(2,1)S(1)} %get-tuple-element.161), channel_id=1, source_target_pairs={{0,24},{4,28},{8,16},{12,20},{16,8},{20,12},{24,0},{28,4},{1,25},{... | collective-permute-start | bytes 1327112 | tf_op jit(solution)/shard_map/ppermute | solution.py:89
  52.7 53.2 %collective-permute-start.20 = (bf16[4,3,96,768]{3,2,1,0:T(8,128)(2,1)}, bf16[4,3,96,768]{3,2,1,0:T(8,128)(2,1)S(1)}, u32[]{:S(2)}, u32[]{:S(2)}) collective-permute-start(bf16[4,3,96,768]{3,2,1,0:T(8,128)(2,1)} %get-tuple-element.135), channel_id=1, source_target_pairs={{0,4},{4,0},{8,12},{12,8},{16,20},{20,16},{24,28},{28,24},{1,5},{5... | collective-permute-start | bytes 5308424 | tf_op jit(solution)/shard_map/ppermute | solution.py:89
  71.7 44.5 %collective-permute-start.13 = (bf16[4,3,96,768]{3,2,1,0:T(8,128)(2,1)}, bf16[4,3,96,768]{3,2,1,0:T(8,128)(2,1)}, u32[]{:S(2)}, u32[]{:S(2)}) collective-permute-start(bf16[4,3,96,768]{3,2,1,0:T(8,128)(2,1)} %get-tuple-element.139), channel_id=1, source_target_pairs={{0,4},{4,0},{8,12},{12,8},{16,20},{20,16},{24,28},{28,24},{1,5},{5... | collective-permute-start | bytes 5308424 | tf_op jit(solution)/shard_map/ppermute | solution.py:89
  77.2 11.9 %collective-permute-start.4 = (bf16[3,96,768]{2,1,0:T(8,128)(2,1)S(1)}, bf16[3,96,768]{2,1,0:T(8,128)(2,1)S(1)}, u32[]{:S(2)}, u32[]{:S(2)}) collective-permute-start(bf16[3,96,768]{2,1,0:T(8,128)(2,1)S(1)} %get-tuple-element.159), channel_id=1, source_target_pairs={{0,16},{4,20},{8,24},{12,28},{16,0},{20,4},{24,8},{28,12},{1,17},{... | collective-permute-start | bytes 1327112 | tf_op jit(solution)/shard_map/ppermute | solution.py:89
  77.5 11.6 %collective-permute-start.3 = (bf16[3,96,768]{2,1,0:T(8,128)(2,1)S(1)}, bf16[3,96,768]{2,1,0:T(8,128)(2,1)S(1)}, u32[]{:S(2)}, u32[]{:S(2)}) collective-permute-start(bf16[3,96,768]{2,1,0:T(8,128)(2,1)S(1)} %get-tuple-element.159), channel_id=1, source_target_pairs={{0,8},{4,12},{8,0},{12,4},{16,24},{20,28},{24,16},{28,20},{1,9},{5... | collective-permute-start | bytes 1327112 | tf_op jit(solution)/shard_map/ppermute | solution.py:89
  78.7 20.7 %collective-permute-start.5 = (bf16[3,96,768]{2,1,0:T(8,128)(2,1)S(1)}, bf16[3,96,768]{2,1,0:T(8,128)(2,1)S(1)}, u32[]{:S(2)}, u32[]{:S(2)}) collective-permute-start(bf16[3,96,768]{2,1,0:T(8,128)(2,1)S(1)} %get-tuple-element.159), channel_id=1, source_target_pairs={{0,24},{4,28},{8,16},{12,20},{16,8},{20,12},{24,0},{28,4},{1,25},{... | collective-permute-start | bytes 1327112 | tf_op jit(solution)/shard_map/ppermute | solution.py:89
  101.5 35.4 %collective-permute-start.6 = (bf16[4,3,96,768]{3,2,1,0:T(8,128)(2,1)}, bf16[4,3,96,768]{3,2,1,0:T(8,128)(2,1)}, u32[]{:S(2)}, u32[]{:S(2)}) collective-permute-start(bf16[4,3,96,768]{3,2,1,0:T(8,128)(2,1)} %get-tuple-element.137), channel_id=1, source_target_pairs={{0,4},{4,0},{8,12},{12,8},{16,20},{20,16},{24,28},{28,24},{1,5},{5... | collective-permute-start | bytes 5308424 | tf_op jit(solution)/shard_map/ppermute | solution.py:89
  103.8 35.1 %copy-start.34 = (s32[1024]{0:T(1024)}, s32[1024]{0:T(1024)S(1)}, u32[]{:S(2)}) copy-start(s32[1024]{0:T(1024)S(1)} %pad_clamp_fusion.3) | copy-start | bytes 12292
  169.4 17.0 %slice-start.7 = ((s8[4718592]{0:T(1024)(128)(4,1)}), s8[4194304]{0:T(1024)(128)(4,1)S(1)}, s32[]{:S(2)}) async-start(s8[4718592]{0:T(1024)(128)(4,1)} %bitcast.382), calls=%async_computation.7 | async-start | bytes 8388608
  212.8 17.1 %slice-start = ((s8[12582912]{0:T(1024)(128)(4,1)}), s8[4194304]{0:T(1024)(128)(4,1)S(1)}, s32[]{:S(2)}) async-start(s8[12582912]{0:T(1024)(128)(4,1)} %bitcast.346), calls=%async_computation | async-start | bytes 8388608
  212.8 17.0 %slice-start.1 = ((s8[12582912]{0:T(1024)(128)(4,1)}), s8[4194304]{0:T(1024)(128)(4,1)S(1)}, s32[]{:S(2)}) async-start(s8[12582912]{0:T(1024)(128)(4,1)} %bitcast.346), calls=%async_computation.1 | async-start | bytes 8388608
  260.7 104.2 %collective-permute-start.45 = (bf16[4,4,96,768]{3,2,1,0:T(8,128)(2,1)}, bf16[4,4,96,768]{3,2,1,0:T(8,128)(2,1)}, u32[]{:S(2)}, u32[]{:S(2)}) collective-permute-start(bf16[4,4,96,768]{3,2,1,0:T(8,128)(2,1)} %slice_bitcast_fusion), channel_id=1, source_target_pairs={{0,4},{4,0},{8,12},{12,8},{16,20},{20,16},{24,28},{28,24},{1,5},{5... | collective-permute-start | bytes 7077896 | tf_op jit(solution)/shard_map/ppermute | solution.py:89
  311.5 61.5 %collective-permute-start.21 = (bf16[4,4,96,768]{3,2,0,1:T(8,128)(2,1)}, bf16[4,4,96,768]{3,2,0,1:T(8,128)(2,1)}, u32[]{:S(2)}, u32[]{:S(2)}) collective-permute-start(bf16[4,4,96,768]{3,2,0,1:T(8,128)(2,1)} %slice_bitcast_fusion.2), channel_id=1, source_target_pairs={{0,4},{4,0},{8,12},{12,8},{16,20},{20,16},{24,28},{28,24},{1,5},{5... | collective-permute-start | bytes 7077896 | tf_op jit(solution)/shard_map/ppermute | solution.py:89
  311.6 47.8 %copy-start.17 = (bf16[12,64,512]{2,1,0:T(8,128)(2,1)S(1)}, bf16[12,64,512]{2,1,0:T(8,128)(2,1)}, u32[]{:S(2)}) copy-start(bf16[12,64,512]{2,1,0:T(8,128)(2,1)} %get-tuple-element.178) | copy-start | bytes 2359300
  311.6 50.0 %copy-start.32 = (bf16[12,64,512]{2,1,0:T(8,128)(2,1)S(1)}, bf16[12,64,512]{2,1,0:T(8,128)(2,1)}, u32[]{:S(2)}) copy-start(bf16[12,64,512]{2,1,0:T(8,128)(2,1)} %multiply_convert_fusion.1) | copy-start | bytes 2359300
  313.2 62.9 %collective-permute-start.33 = (bf16[4,4,96,768]{3,2,1,0:T(8,128)(2,1)}, bf16[4,4,96,768]{3,2,1,0:T(8,128)(2,1)}, u32[]{:S(2)}, u32[]{:S(2)}) collective-permute-start(bf16[4,4,96,768]{3,2,1,0:T(8,128)(2,1)} %slice_bitcast_fusion.1), channel_id=1, source_target_pairs={{0,4},{4,0},{8,12},{12,8},{16,20},{20,16},{24,28},{28,24},{1,5},{5... | collective-permute-start | bytes 7077896 | tf_op jit(solution)/shard_map/ppermute | solution.py:89
  369.1 26.6 %collective-permute-start.48 = (bf16[4,2,96,384]{3,2,1,0:T(8,128)(2,1)}, bf16[4,2,96,384]{3,2,1,0:T(8,128)(2,1)}, u32[]{:S(2)}, u32[]{:S(2)}) collective-permute-start(bf16[4,2,96,384]{3,2,1,0:T(8,128)(2,1)} %slice.423), channel_id=1, source_target_pairs={{0,16},{4,20},{8,24},{12,28},{16,0},{20,4},{24,8},{28,12},{1,17},{... | collective-permute-start | bytes 1769480 | tf_op jit(solution)/shard_map/ppermute | solution.py:89
  372.7 24.7 %collective-permute-start.46 = (bf16[4,2,96,384]{3,2,0,1:T(8,128)(2,1)}, bf16[4,2,96,384]{3,2,0,1:T(8,128)(2,1)}, u32[]{:S(2)}, u32[]{:S(2)}) collective-permute-start(bf16[4,2,96,384]{3,2,0,1:T(8,128)(2,1)} %bitcast.161), channel_id=1, source_target_pairs={{0,8},{4,12},{8,0},{12,4},{16,24},{20,28},{24,16},{28,20},{1,9},{5... | collective-permute-start | bytes 1769480 | tf_op jit(solution)/shard_map/ppermute | solution.py:89
  393.0 12.1 %collective-permute-start.36 = (bf16[4,2,96,384]{3,2,1,0:T(8,128)(2,1)}, bf16[4,2,96,384]{3,2,1,0:T(8,128)(2,1)S(1)}, u32[]{:S(2)}, u32[]{:S(2)}) collective-permute-start(bf16[4,2,96,384]{3,2,1,0:T(8,128)(2,1)} %slice.408), channel_id=1, source_target_pairs={{0,16},{4,20},{8,24},{12,28},{16,0},{20,4},{24,8},{28,12},{1,17},{... | collective-permute-start | bytes 1769480 | tf_op jit(solution)/shard_map/ppermute | solution.py:89
  394.2 14.3 %collective-permute-start.34 = (bf16[4,2,96,384]{3,2,0,1:T(8,128)(2,1)}, bf16[4,2,96,384]{3,2,0,1:T(8,128)(2,1)S(1)}, u32[]{:S(2)}, u32[]{:S(2)}) collective-permute-start(bf16[4,2,96,384]{3,2,0,1:T(8,128)(2,1)} %bitcast.421), channel_id=1, source_target_pairs={{0,8},{4,12},{8,0},{12,4},{16,24},{20,28},{24,16},{28,20},{1,9},{5... | collective-permute-start | bytes 1769480 | tf_op jit(solution)/shard_map/ppermute | solution.py:89
  394.3 23.5 %collective-permute-start.24 = (bf16[4,2,96,384]{3,2,0,1:T(8,128)(2,1)}, bf16[4,2,96,384]{3,2,0,1:T(8,128)(2,1)S(1)}, u32[]{:S(2)}, u32[]{:S(2)}) collective-permute-start(bf16[4,2,96,384]{3,2,0,1:T(8,128)(2,1)} %slice.386), channel_id=1, source_target_pairs={{0,16},{4,20},{8,24},{12,28},{16,0},{20,4},{24,8},{28,12},{1,17},{... | collective-permute-start | bytes 1769480 | tf_op jit(solution)/shard_map/ppermute | solution.py:89
  395.7 24.4 %collective-permute-start.22 = (bf16[4,2,96,384]{3,2,0,1:T(8,128)(2,1)}, bf16[4,2,96,384]{3,2,0,1:T(8,128)(2,1)S(1)}, u32[]{:S(2)}, u32[]{:S(2)}) collective-permute-start(bf16[4,2,96,384]{3,2,0,1:T(8,128)(2,1)} %bitcast.420), channel_id=1, source_target_pairs={{0,8},{4,12},{8,0},{12,4},{16,24},{20,28},{24,16},{28,20},{1,9},{5... | collective-permute-start | bytes 1769480 | tf_op jit(solution)/shard_map/ppermute | solution.py:89
  397.4 28.5 %collective-permute-start.49 = (bf16[4,96,384]{2,1,0:T(8,128)(2,1)S(1)}, bf16[4,96,384]{2,1,0:T(8,128)(2,1)S(1)}, u32[]{:S(2)}, u32[]{:S(2)}) collective-permute-start(bf16[4,96,384]{2,1,0:T(8,128)(2,1)S(1)} %slice_bitcast_fusion.5), channel_id=1, source_target_pairs={{0,8},{4,12},{8,0},{12,4},{16,24},{20,28},{24,16},{28,20},{1,9},{5... | collective-permute-start | bytes 884744 | tf_op jit(solution)/shard_map/ppermute | solution.py:89
  405.2 20.9 %collective-permute-start.47 = (bf16[4,96,384]{2,1,0:T(8,128)(2,1)S(1)}, bf16[4,96,384]{2,1,0:T(8,128)(2,1)S(1)}, u32[]{:S(2)}, u32[]{:S(2)}) collective-permute-start(bf16[4,96,384]{2,1,0:T(8,128)(2,1)S(1)} %slice_bitcast_fusion.7), channel_id=1, source_target_pairs={{0,16},{4,20},{8,24},{12,28},{16,0},{20,4},{24,8},{28,12},{1,17},{... | collective-permute-start | bytes 884744 | tf_op jit(solution)/shard_map/ppermute | solution.py:89
  408.5 23.7 %collective-permute-start.37 = (bf16[4,96,384]{2,1,0:T(8,128)(2,1)S(1)}, bf16[4,96,384]{2,1,0:T(8,128)(2,1)S(1)}, u32[]{:S(2)}, u32[]{:S(2)}) collective-permute-start(bf16[4,96,384]{2,1,0:T(8,128)(2,1)S(1)} %slice_bitcast_fusion.9), channel_id=1, source_target_pairs={{0,8},{4,12},{8,0},{12,4},{16,24},{20,28},{24,16},{28,20},{1,9},{5... | collective-permute-start | bytes 884744 | tf_op jit(solution)/shard_map/ppermute | solution.py:89
  417.8 14.5 %collective-permute-start.35 = (bf16[4,96,384]{2,1,0:T(8,128)(2,1)S(1)}, bf16[4,96,384]{2,1,0:T(8,128)(2,1)S(1)}, u32[]{:S(2)}, u32[]{:S(2)}) collective-permute-start(bf16[4,96,384]{2,1,0:T(8,128)(2,1)S(1)} %slice_bitcast_fusion.11), channel_id=1, source_target_pairs={{0,16},{4,20},{8,24},{12,28},{16,0},{20,4},{24,8},{28,12},{1,17},{... | collective-permute-start | bytes 884744 | tf_op jit(solution)/shard_map/ppermute | solution.py:89
  420.1 18.5 %collective-permute-start.25 = (bf16[4,96,384]{2,1,0:T(8,128)(2,1)S(1)}, bf16[4,96,384]{2,1,0:T(8,128)(2,1)S(1)}, u32[]{:S(2)}, u32[]{:S(2)}) collective-permute-start(bf16[4,96,384]{2,1,0:T(8,128)(2,1)S(1)} %slice_bitcast_fusion.13), channel_id=1, source_target_pairs={{0,8},{4,12},{8,0},{12,4},{16,24},{20,28},{24,16},{28,20},{1,9},{5... | collective-permute-start | bytes 884744 | tf_op jit(solution)/shard_map/ppermute | solution.py:89
  425.9 31.8 %collective-permute-start.23 = (bf16[4,96,384]{2,1,0:T(8,128)(2,1)S(1)}, bf16[4,96,384]{2,1,0:T(8,128)(2,1)S(1)}, u32[]{:S(2)}, u32[]{:S(2)}) collective-permute-start(bf16[4,96,384]{2,1,0:T(8,128)(2,1)S(1)} %slice_bitcast_fusion.15), channel_id=1, source_target_pairs={{0,16},{4,20},{8,24},{12,28},{16,0},{20,4},{24,8},{28,12},{1,17},{... | collective-permute-start | bytes 884744 | tf_op jit(solution)/shard_map/ppermute | solution.py:89
  426.2 14.5 %collective-permute-start.50 = (bf16[96,768]{1,0:T(8,128)(2,1)S(1)}, bf16[96,768]{1,0:T(8,128)(2,1)S(1)}, u32[]{:S(2)}, u32[]{:S(2)}) collective-permute-start(bf16[96,768]{1,0:T(8,128)(2,1)S(1)} %get-tuple-element.143), channel_id=1, source_target_pairs={{0,3},{1,0},{2,1},{3,2},{4,7},{5,4},{6,5},{7,6},{8,11},{9,8},{10,9... | collective-permute-start | bytes 442376 | tf_op jit(solution)/shard_map/ppermute | solution.py:86
  432.3 8.5 %collective-permute-start.52 = (bf16[96,768]{1,0:T(8,128)(2,1)S(1)}, bf16[96,768]{1,0:T(8,128)(2,1)S(1)}, u32[]{:S(2)}, u32[]{:S(2)}) collective-permute-start(bf16[96,768]{1,0:T(8,128)(2,1)S(1)} %get-tuple-element.144), channel_id=1, source_target_pairs={{0,1},{1,2},{2,3},{3,0},{4,5},{5,6},{6,7},{7,4},{8,9},{9,10},{10,1... | collective-permute-start | bytes 442376 | tf_op jit(solution)/shard_map/ppermute | solution.py:86
  432.4 9.4 %collective-permute-start.51 = (bf16[96,768]{1,0:T(8,128)(2,1)S(1)}, bf16[96,768]{1,0:T(8,128)(2,1)S(1)}, u32[]{:S(2)}, u32[]{:S(2)}) collective-permute-start(bf16[96,768]{1,0:T(8,128)(2,1)S(1)} %get-tuple-element.145), channel_id=1, source_target_pairs={{0,2},{1,3},{2,0},{3,1},{4,6},{5,7},{6,4},{7,5},{8,10},{9,11},{10,... | collective-permute-start | bytes 442376 | tf_op jit(solution)/shard_map/ppermute | solution.py:86
  438.6 6.6 %collective-permute-start.38 = (bf16[96,768]{1,0:T(8,128)(2,1)S(1)}, bf16[96,768]{1,0:T(8,128)(2,1)S(1)}, u32[]{:S(2)}, u32[]{:S(2)}) collective-permute-start(bf16[96,768]{1,0:T(8,128)(2,1)S(1)} %get-tuple-element.148), channel_id=1, source_target_pairs={{0,3},{1,0},{2,1},{3,2},{4,7},{5,4},{6,5},{7,6},{8,11},{9,8},{10,9... | collective-permute-start | bytes 442376 | tf_op jit(solution)/shard_map/ppermute | solution.py:86
  440.7 7.5 %collective-permute-start.40 = (bf16[96,768]{1,0:T(8,128)(2,1)S(1)}, bf16[96,768]{1,0:T(8,128)(2,1)S(1)}, u32[]{:S(2)}, u32[]{:S(2)}) collective-permute-start(bf16[96,768]{1,0:T(8,128)(2,1)S(1)} %get-tuple-element.149), channel_id=1, source_target_pairs={{0,1},{1,2},{2,3},{3,0},{4,5},{5,6},{6,7},{7,4},{8,9},{9,10},{10,1... | collective-permute-start | bytes 442376 | tf_op jit(solution)/shard_map/ppermute | solution.py:86
  440.7 16.9 %collective-permute-start.39 = (bf16[96,768]{1,0:T(8,128)(2,1)S(1)}, bf16[96,768]{1,0:T(8,128)(2,1)S(1)}, u32[]{:S(2)}, u32[]{:S(2)}) collective-permute-start(bf16[96,768]{1,0:T(8,128)(2,1)S(1)} %get-tuple-element.150), channel_id=1, source_target_pairs={{0,2},{1,3},{2,0},{3,1},{4,6},{5,7},{6,4},{7,5},{8,10},{9,11},{10,... | collective-permute-start | bytes 442376 | tf_op jit(solution)/shard_map/ppermute | solution.py:86
  441.9 17.6 %collective-permute-start.55 = (bf16[96,768]{1,0:T(8,128)(2,1)S(1)}, bf16[96,768]{1,0:T(8,128)(2,1)S(1)}, u32[]{:S(2)}, u32[]{:S(2)}) collective-permute-start(bf16[96,768]{1,0:T(8,128)(2,1)S(1)} %fusion.58), channel_id=1, source_target_pairs={{0,24},{4,28},{8,16},{12,20},{16,8},{20,12},{24,0},{28,4},{1,25},{... | collective-permute-start | bytes 442376 | tf_op jit(solution)/shard_map/ppermute | solution.py:89
  445.2 15.4 %collective-permute-start.54 = (bf16[96,768]{1,0:T(8,128)(2,1)S(1)}, bf16[96,768]{1,0:T(8,128)(2,1)S(1)}, u32[]{:S(2)}, u32[]{:S(2)}) collective-permute-start(bf16[96,768]{1,0:T(8,128)(2,1)S(1)} %fusion.58), channel_id=1, source_target_pairs={{0,16},{4,20},{8,24},{12,28},{16,0},{20,4},{24,8},{28,12},{1,17},{... | collective-permute-start | bytes 442376 | tf_op jit(solution)/shard_map/ppermute | solution.py:89
  448.2 13.8 %collective-permute-start.53 = (bf16[96,768]{1,0:T(8,128)(2,1)S(1)}, bf16[96,768]{1,0:T(8,128)(2,1)S(1)}, u32[]{:S(2)}, u32[]{:S(2)}) collective-permute-start(bf16[96,768]{1,0:T(8,128)(2,1)S(1)} %fusion.58), channel_id=1, source_target_pairs={{0,8},{4,12},{8,0},{12,4},{16,24},{20,28},{24,16},{28,20},{1,9},{5... | collective-permute-start | bytes 442376 | tf_op jit(solution)/shard_map/ppermute | solution.py:89
  457.7 6.6 %collective-permute-start.43 = (bf16[96,768]{1,0:T(8,128)(2,1)S(1)}, bf16[96,768]{1,0:T(8,128)(2,1)S(1)}, u32[]{:S(2)}, u32[]{:S(2)}) collective-permute-start(bf16[96,768]{1,0:T(8,128)(2,1)S(1)} %fusion.61), channel_id=1, source_target_pairs={{0,24},{4,28},{8,16},{12,20},{16,8},{20,12},{24,0},{28,4},{1,25},{... | collective-permute-start | bytes 442376 | tf_op jit(solution)/shard_map/ppermute | solution.py:89
  457.9 10.1 %collective-permute-start.42 = (bf16[96,768]{1,0:T(8,128)(2,1)S(1)}, bf16[96,768]{1,0:T(8,128)(2,1)S(1)}, u32[]{:S(2)}, u32[]{:S(2)}) collective-permute-start(bf16[96,768]{1,0:T(8,128)(2,1)S(1)} %fusion.61), channel_id=1, source_target_pairs={{0,16},{4,20},{8,24},{12,28},{16,0},{20,4},{24,8},{28,12},{1,17},{... | collective-permute-start | bytes 442376 | tf_op jit(solution)/shard_map/ppermute | solution.py:89
  459.5 11.0 %collective-permute-start.41 = (bf16[96,768]{1,0:T(8,128)(2,1)S(1)}, bf16[96,768]{1,0:T(8,128)(2,1)S(1)}, u32[]{:S(2)}, u32[]{:S(2)}) collective-permute-start(bf16[96,768]{1,0:T(8,128)(2,1)S(1)} %fusion.61), channel_id=1, source_target_pairs={{0,8},{4,12},{8,0},{12,4},{16,24},{20,28},{24,16},{28,20},{1,9},{5... | collective-permute-start | bytes 442376 | tf_op jit(solution)/shard_map/ppermute | solution.py:89
  460.6 10.1 %collective-permute-start.26 = (bf16[96,768]{1,0:T(8,128)(2,1)S(1)}, bf16[96,768]{1,0:T(8,128)(2,1)S(1)}, u32[]{:S(2)}, u32[]{:S(2)}) collective-permute-start(bf16[96,768]{1,0:T(8,128)(2,1)S(1)} %get-tuple-element.153), channel_id=1, source_target_pairs={{0,3},{1,0},{2,1},{3,2},{4,7},{5,4},{6,5},{7,6},{8,11},{9,8},{10,9... | collective-permute-start | bytes 442376 | tf_op jit(solution)/shard_map/ppermute | solution.py:86
  462.0 8.7 %collective-permute-start.28 = (bf16[96,768]{1,0:T(8,128)(2,1)S(1)}, bf16[96,768]{1,0:T(8,128)(2,1)S(1)}, u32[]{:S(2)}, u32[]{:S(2)}) collective-permute-start(bf16[96,768]{1,0:T(8,128)(2,1)S(1)} %get-tuple-element.154), channel_id=1, source_target_pairs={{0,1},{1,2},{2,3},{3,0},{4,5},{5,6},{6,7},{7,4},{8,9},{9,10},{10,1... | collective-permute-start | bytes 442376 | tf_op jit(solution)/shard_map/ppermute | solution.py:86
  464.3 8.4 %collective-permute-start.27 = (bf16[96,768]{1,0:T(8,128)(2,1)S(1)}, bf16[96,768]{1,0:T(8,128)(2,1)S(1)}, u32[]{:S(2)}, u32[]{:S(2)}) collective-permute-start(bf16[96,768]{1,0:T(8,128)(2,1)S(1)} %get-tuple-element.155), channel_id=1, source_target_pairs={{0,2},{1,3},{2,0},{3,1},{4,6},{5,7},{6,4},{7,5},{8,10},{9,11},{10,... | collective-permute-start | bytes 442376 | tf_op jit(solution)/shard_map/ppermute | solution.py:86
  467.9 20.0 %collective-permute-start.56 = (bf16[4,96,768]{2,1,0:T(8,128)(2,1)S(1)}, bf16[4,96,768]{2,1,0:T(8,128)(2,1)S(1)}, u32[]{:S(2)}, u32[]{:S(2)}) collective-permute-start(bf16[4,96,768]{2,1,0:T(8,128)(2,1)S(1)} %get-tuple-element.142), channel_id=1, source_target_pairs={{0,4},{4,0},{8,12},{12,8},{16,20},{20,16},{24,28},{28,24},{1,5},{5... | collective-permute-start | bytes 1769480 | tf_op jit(solution)/shard_map/ppermute | solution.py:89
  470.6 18.1 %collective-permute-start.44 = (bf16[4,96,768]{2,1,0:T(8,128)(2,1)S(1)}, bf16[4,96,768]{2,1,0:T(8,128)(2,1)}, u32[]{:S(2)}, u32[]{:S(2)}) collective-permute-start(bf16[4,96,768]{2,1,0:T(8,128)(2,1)S(1)} %get-tuple-element.147), channel_id=1, source_target_pairs={{0,4},{4,0},{8,12},{12,8},{16,20},{20,16},{24,28},{28,24},{1,5},{5... | collective-permute-start | bytes 1769480 | tf_op jit(solution)/shard_map/ppermute | solution.py:89
  472.7 6.1 %collective-permute-start.31 = (bf16[96,768]{1,0:T(8,128)(2,1)S(1)}, bf16[96,768]{1,0:T(8,128)(2,1)S(1)}, u32[]{:S(2)}, u32[]{:S(2)}) collective-permute-start(bf16[96,768]{1,0:T(8,128)(2,1)S(1)} %fusion.64), channel_id=1, source_target_pairs={{0,24},{4,28},{8,16},{12,20},{16,8},{20,12},{24,0},{28,4},{1,25},{... | collective-permute-start | bytes 442376 | tf_op jit(solution)/shard_map/ppermute | solution.py:89
  473.0 5.9 %collective-permute-start.30 = (bf16[96,768]{1,0:T(8,128)(2,1)S(1)}, bf16[96,768]{1,0:T(8,128)(2,1)S(1)}, u32[]{:S(2)}, u32[]{:S(2)}) collective-permute-start(bf16[96,768]{1,0:T(8,128)(2,1)S(1)} %fusion.64), channel_id=1, source_target_pairs={{0,16},{4,20},{8,24},{12,28},{16,0},{20,4},{24,8},{28,12},{1,17},{... | collective-permute-start | bytes 442376 | tf_op jit(solution)/shard_map/ppermute | solution.py:89
  474.7 4.2 collective-permute-start.29
  480.0 14.0 %collective-permute-start.32 = (bf16[4,96,768]{2,1,0:T(8,128)(2,1)}, bf16[4,96,768]{2,1,0:T(8,128)(2,1)}, u32[]{:S(2)}, u32[]{:S(2)}) collective-permute-start(bf16[4,96,768]{2,1,0:T(8,128)(2,1)} %get-tuple-element.152), channel_id=1, source_target_pairs={{0,4},{4,0},{8,12},{12,8},{16,20},{20,16},{24,28},{28,24},{1,5},{5... | collective-permute-start | bytes 1769480 | tf_op jit(solution)/shard_map/ppermute | solution.py:89
  (56 other events, 267.8 us)
where the time goes:
time: 509 us; the launch traced here: 501 us
  local copies, waits for them, and re-layouts  131 us (26%)
  waiting for transfers between devices  88.2 us (17%)
  matrix products  84.6 us (17%)
  starting transfers between devices  79 us (16%)
  other arithmetic  71.9 us (14%)
  blocking collectives  44.2 us (9%)
    ppermute x39, waiting for transfers between devices, swap(): return lax.ppermute(array, 'dp', [(i, i ^ bits) for i in range(n_dp)])  59.2 us
    ppermute x39, starting transfers between devices, swap(): return lax.ppermute(array, 'dp', [(i, i ^ bits) for i in range(n_dp)])  55.1 us
    psum x1, blocking collectives, shards(): mine, shared = lax.psum((mine, shared), ('dp', 'mp'))  44.2 us
    ppermute x18, waiting for transfers between devices, rotate(): lax.ppermute(array, 'mp', [(i, (i + step) % n_mp) for i in range(n_mp)])  29 us
    dot_general x6, matrix products, mm(): return jnp.dot(left, right, preferred_element_type=f32)  23.9 us
    ppermute x18, starting transfers between devices, rotate(): lax.ppermute(array, 'mp', [(i, (i + step) % n_mp) for i in range(n_mp)])  23.9 us
    gather x5, local copies, waits for them, and re-layouts, reduce_grads(): slots = grads.astype(bf16).reshape(quarters, GROUP, rows, width)[:, order]  23.6 us
    dot_general x6, matrix products, inner_rows(): lax.dot_general(left, right, (((0,), (0,)), ((), ())), preferred_element_...  19.5 us
  transfers between devices with their start and end apart: 57, of which 19 were waited for; matrix products, arithmetic and copies ran while one was open for 30% of the time, Pallas kernels for 0%

commit v1 on v0

--- a/solution.py
+++ b/solution.py
@@ -281,7 +281,7 @@
                 grad_second_shift,
             ]
         )
-        mine, shared = lax.psum((mine, shared), ("dp", "mp"))
+        mine, shared = lax.psum(lax.psum((mine, shared), "mp"), "dp")
         mine = lax.dynamic_index_in_dim(mine, place, 0, keepdims=False)
         return (
             result.astype(bf16),

time: 509 us -> 507 us (level)
  starting transfers between devices: 79 us -> 73.8 us
    ppermute x39, waiting for transfers between devices: 59.2 us -> 64.9 us  [swap(): return lax.ppermute(array, 'dp', [(i, i ^ bits) for i in range(n_dp)])]
    psum x1 -> x2, blocking collectives: 44.2 us -> 42.7 us  [shards(): mine, shared = lax.psum(lax.psum((mine, shared), 'mp'), 'dp')]
  transfers between devices with their start and end apart: 57 -> 57, of which waited for: 19 -> 20; matrix products, arithmetic and copies ran while one was open for 30% -> 31% of each run, Pallas kernels for 0% -> 0%
where the time goes in v1:
time: 507 us; the launch traced here: 499 us
  local copies, waits for them, and re-layouts  131 us (26%)
  waiting for transfers between devices  92.7 us (18%)
  matrix products  84.6 us (17%)
  starting transfers between devices  73.8 us (15%)
  other arithmetic  72 us (14%)
  blocking collectives  42.7 us (8%)
    ppermute x39, waiting for transfers between devices, swap(): return lax.ppermute(array, 'dp', [(i, i ^ bits) for i in range(n_dp)])  64.9 us
    ppermute x39, starting transfers between devices, swap(): return lax.ppermute(array, 'dp', [(i, i ^ bits) for i in range(n_dp)])  52.9 us
    psum x2, blocking collectives, shards(): mine, shared = lax.psum(lax.psum((mine, shared), 'mp'), 'dp')  42.7 us
    ppermute x18, waiting for transfers between devices, rotate(): lax.ppermute(array, 'mp', [(i, (i + step) % n_mp) for i in range(n_mp)])  27.9 us
    dot_general x6, matrix products, mm(): return jnp.dot(left, right, preferred_element_type=f32)  23.9 us
    gather x5, local copies, waits for them, and re-layouts, reduce_grads(): slots = grads.astype(bf16).reshape(quarters, GROUP, rows, width)[:, order]  23.7 us
    ppermute x18, starting transfers between devices, rotate(): lax.ppermute(array, 'mp', [(i, (i + step) % n_mp) for i in range(n_mp)])  20.9 us
    dot_general x6, matrix products, inner_rows(): lax.dot_general(left, right, (((0,), (0,)), ((), ())), preferred_element_...  19.5 us
  transfers between devices with their start and end apart: 57, of which 20 were waited for; matrix products, arithmetic and copies ran while one was open for 31% of the time, Pallas kernels for 0%

profile of v1, /device:TPU:1, one launch (start us, length us, event | category | flops | bytes accessed | tf_op | source)
XLA Modules:
  0.0 499.1 jit_solution(9360616359031152209)
XLA Ops:
  1.7 4.2 collective-permute-start.16
  7.3 2.9 collective-permute-start.9
  21.3 3.2 collective-permute-start.2
  35.7 8.9 %collective-permute-done.1 = bf16[104,768]{1,0:T(8,128)(2,1)S(1)} collective-permute-done((bf16[104,768]{1,0:T(8,128)(2,1)S(1)}, bf16[104,768]{1,0:T(8,128)(2,1)S(1)}, u32[]{:S(2)}, u32[]{:S(2)}) %collective-permute-start.1) | collective-permute-done | bytes 159776 | tf_op jit(solution)/shard_map/ppermute | solution.py:86
  47.3 3.4 collective-permute-done.19
  52.7 10.4 %collective-permute-start.20 = (bf16[4,3,96,768]{3,2,1,0:T(8,128)(2,1)}, bf16[4,3,96,768]{3,2,1,0:T(8,128)(2,1)S(1)}, u32[]{:S(2)}, u32[]{:S(2)}) collective-permute-start(bf16[4,3,96,768]{3,2,1,0:T(8,128)(2,1)} %get-tuple-element.137), channel_id=1, source_target_pairs={{0,4},{4,0},{8,12},{12,8},{16,20},{20,16},{24,28},{28,24},{1,5},{5... | collective-permute-start | bytes 5308424 | tf_op jit(solution)/shard_map/ppermute | solution.py:89
  64.5 5.1 %collective-permute-done.12 = bf16[3,96,768]{2,1,0:T(8,128)(2,1)S(1)} collective-permute-done((bf16[3,96,768]{2,1,0:T(8,128)(2,1)S(1)}, bf16[3,96,768]{2,1,0:T(8,128)(2,1)S(1)}, u32[]{:S(2)}, u32[]{:S(2)}) %collective-permute-start.12) | collective-permute-done | bytes 442400 | tf_op jit(solution)/shard_map/ppermute | solution.py:89
  71.7 5.5 %collective-permute-start.13 = (bf16[4,3,96,768]{3,2,1,0:T(8,128)(2,1)}, bf16[4,3,96,768]{3,2,1,0:T(8,128)(2,1)}, u32[]{:S(2)}, u32[]{:S(2)}) collective-permute-start(bf16[4,3,96,768]{3,2,1,0:T(8,128)(2,1)} %get-tuple-element.141), channel_id=1, source_target_pairs={{0,4},{4,0},{8,12},{12,8},{16,20},{20,16},{24,28},{28,24},{1,5},{5... | collective-permute-start | bytes 5308424 | tf_op jit(solution)/shard_map/ppermute | solution.py:89
  82.5 6.6 %collective-permute-done.4 = bf16[3,96,768]{2,1,0:T(8,128)(2,1)S(1)} collective-permute-done((bf16[3,96,768]{2,1,0:T(8,128)(2,1)S(1)}, bf16[3,96,768]{2,1,0:T(8,128)(2,1)S(1)}, u32[]{:S(2)}, u32[]{:S(2)}) %collective-permute-start.4) | collective-permute-done | bytes 442400 | tf_op jit(solution)/shard_map/ppermute | solution.py:89
  89.1 10.3 %collective-permute-done.5 = bf16[3,96,768]{2,1,0:T(8,128)(2,1)S(1)} collective-permute-done((bf16[3,96,768]{2,1,0:T(8,128)(2,1)S(1)}, bf16[3,96,768]{2,1,0:T(8,128)(2,1)S(1)}, u32[]{:S(2)}, u32[]{:S(2)}) %collective-permute-start.5) | collective-permute-done | bytes 442400 | tf_op jit(solution)/shard_map/ppermute | solution.py:89
  109.5 2.5 gather_fusion.2
  112.0 4.2 copy.146
  118.0 2.5 gather_fusion.1
  122.9 2.6 maximum_bitcast_fusion
  125.5 7.4 %copy.144 = bf16[768,4,768]{0,2,1:T(8,128)(2,1)} copy(bf16[768,4,768]{2,0,1:T(8,128)(2,1)} %maximum_bitcast_fusion) | data formatting | bytes 9437184 | tf_op jit(solution)/shard_map/transpose | solution.py:179
  132.9 4.0 pad_maximum_fusion
  138.9 2.5 gather_fusion
  143.8 2.9 fusion.39
  146.8 2.5 copy.141
  149.2 2.5 copy.137
  160.0 2.6 fusion
  165.6 3.8 fusion.44
  170.8 15.7 %fusion.4 = (bf16[512,3072]{1,0:T(8,128)(2,1)S(1)}, f32[512,3072]{1,0:T(8,128)S(1)}) fusion(f32[3072]{0:T(1024)S(1)} %bitcast.450, bf16[768,3072]{0,1:T(8,128)(2,1)S(1)} %bitcast.380, f32[512,768]{1,0:T(8,128)S(1)} %get-tuple-element.171, f32[768]{0:T(1024)S(1)} %copy-done.38, f32[768]{0:T(1024)S(1)} %convert_element_type.401, f32[512]{0:T(512)S(1)} %add_rsqrt_fusion.1, ...), kind=kOutput, calls=%fused_computation.31 | convolution fusion | flops 2521694208 | bytes 15751168 | tf_op jit(solution)/shard_map/dot_general | solution.py:197
  186.5 2.7 fusion.116
  191.9 4.6 convert_reduce_fusion
  196.6 3.0 multiply_reduce_fusion.1
  199.6 5.2 %convolution_convert_fusion.1 = bf16[768,3072]{1,0:T(8,128)(2,1)} fusion(bf16[512,3072]{1,0:T(8,128)(2,1)S(1)} %get-tuple-element.184, f32[512,768]{1,0:T(8,128)S(1)} %get-tuple-element.171, f32[768]{0:T(1024)S(1)} %copy-done.38, f32[768]{0:T(1024)S(1)} %convert_element_type.401, f32[512]{0:T(512)S(1)} %add_rsqrt_fusion.1, f32[512]{0:T(512)S(1)} %broadcast_multiply_fusion.5), kind=kOutput, calls=%fused_computation.58 | convolution fusion | flops 2420244480 | bytes 9447424 | tf_op jit(solution)/shard_map/dot_general | solution.py:15
  204.8 4.3 convolution_convert_fusion
  212.8 7.4 %convert_reduce_fusion.4 = (f32[12,64]{1,0:T(8,128)S(1)}, bf16[12,64,512]{2,1,0:T(8,128)(2,1)}) fusion(bf16[512,12,64]{0,2,1:T(8,128)(2,1)S(1)} %bitcast.391, f32[12,512]{1,0:T(8,128)S(1)} %log_add_fusion, f32[12,512,512]{1,2,0:T(8,128)} %copy-done.2, pred[512,512]{0,1:T(8,128)(4,1)S(1)} %copy-done.9), kind=kOutput, calls=%fused_computation.105 | convolution fusion | flops 416414976 | bytes 14445568 | tf_op jit(solution)/shard_map/hqk,qhd->khd/dot_general | solution.py:66
  220.2 9.6 %multiply_reduce_fusion = (f32[12,512]{1,0:T(8,128)S(1)}, f32[12,512,512]{1,2,0:T(8,128)}) fusion(f32[12,512]{1,0:T(8,128)S(1)} %log_add_fusion, f32[12,512,512]{1,2,0:T(8,128)} %copy-done.2, pred[512,512]{0,1:T(8,128)(4,1)S(1)} %copy-done.9, bf16[512,12,64]{0,2,1:T(8,128)(2,1)S(1)} %bitcast.392, bf16[512,12,64]{0,2,1:T(8,128)(2,1)S(1)} %bitcast.410), kind=kOutput, calls=%fused_computation.17 | convolution fusion | flops 418375680 | bytes 27049984 | tf_op jit(solution)/shard_map/qhd,khd->hqk/dot_general | solution.py:65
  229.8 6.8 %multiply_convert_fusion = bf16[12,512,512]{1,2,0:T(8,128)(2,1)S(1)} fusion(f32[12,512,512]{1,2,0:T(8,128)} %get-tuple-element.178, f32[12,512]{1,0:T(8,128)S(1)} %get-tuple-element.177, f32[12,512]{1,0:T(8,128)S(1)} %log_add_fusion, f32[12,512,512]{1,2,0:T(8,128)S(1)} %bitcast.347, pred[512,512]{0,1:T(8,128)(4,1)S(1)} %copy-done.9), kind=kLoop, calls=%fused_computation.16 | loop fusion | flops 18874368 | bytes 31768576 | tf_op jit(solution)/shard_map/convert_element_type | solution.py:70
  236.7 3.0 multiply_convert_fusion.1
  245.3 3.2 convolution_convert_fusion.3
  248.5 2.5 copy.153
  251.0 5.4 %gather_fusion.12 = bf16[8,4,96,768]{3,2,1,0:T(8,128)(2,1)} fusion(bf16[4,8,96,768]{3,2,1,0:T(8,128)(2,1)} %bitcast.386, s32[1024]{0:T(1024)S(1)} %copy-done.35), kind=kCustom, calls=%fused_computation.12 | custom fusion | bytes 9437216 | tf_op jit(solution)/shard_map/gather | solution.py:114
  256.3 2.7 copy.166
  262.8 2.5 copy.151
  265.3 3.2 convolution_convert_fusion.4
  268.6 2.5 copy.152
  271.1 6.6 %pad_maximum_fusion.1 = bf16[4,8,96,768]{3,2,1,0:T(8,128)(2,1)} fusion(bf16[4,8,96,192]{3,2,1,0:T(8,128)(2,1)S(1)} %bitcast.371, bf16[4,8,96,192]{3,2,1,0:T(8,128)(2,1)} %bitcast.372, bf16[4,8,96,192]{3,2,1,0:T(8,128)(2,1)} %bitcast.374, bf16[4,8,96,192]{3,2,1,0:T(8,128)(2,1)} %bitcast.373), kind=kLoop, calls=%fused_computation.64 | loop fusion | flops 18874368 | bytes 9437184 | tf_op jit(solution)/shard_map/concatenate | solution.py:249
  277.6 9.7 %convert_element_type.455 = bf16[768,4,768]{2,1,0:T(4,128)(2,1)} reshape(bf16[768,3072]{1,0:T(8,128)(2,1)} %convolution_convert_fusion.1) | data formatting | bytes 9437184 | tf_op jit(solution)/shard_map/convert_element_type | solution.py:114
  287.4 5.1 %copy.161 = bf16[4,768,768]{2,1,0:T(8,128)(2,1)} copy(bf16[4,768,768]{2,0,1:T(4,128)(2,1)} %bitcast.356) | data formatting | bytes 9437184 | tf_op jit(solution)/shard_map/convert_element_type | solution.py:114
  292.5 5.4 %gather_fusion.8 = bf16[8,4,96,768]{3,2,1,0:T(8,128)(2,1)} fusion(bf16[4,8,96,768]{3,2,1,0:T(8,128)(2,1)} %bitcast.357, s32[1024]{0:T(1024)S(1)} %copy-done.35), kind=kCustom, calls=%fused_computation.8 | custom fusion | bytes 9437216 | tf_op jit(solution)/shard_map/gather | solution.py:114
  297.9 4.8 copy.162
  302.7 5.4 %gather_fusion.3 = bf16[8,4,96,768]{3,2,1,0:T(8,128)(2,1)} fusion(bf16[4,8,96,768]{3,2,1,0:T(8,128)(2,1)} %pad_maximum_fusion.1, s32[1024]{0:T(1024)S(1)} %copy-done.35), kind=kCustom, calls=%fused_computation.3 | custom fusion | bytes 9437216 | tf_op jit(solution)/shard_map/gather | solution.py:114
  308.1 3.4 slice_bitcast_fusion.2
  315.2 17.8 %all-reduce.2 = (f32[4,1152]{1,0:T(4,128)S(1)}, f32[6,768]{1,0:T(8,128)S(1)}) all-reduce(f32[4,1152]{1,0:T(4,128)S(1)} %gather_fusion.7, f32[6,768]{1,0:T(8,128)S(1)} %stack.271), channel_id=1, replica_groups=mesh['dp'=8,'mp'=4] {'mp'}, use_global_device_ids=true, to_apply=%region_15.16 | all-reduce | flops 9216 | bytes 73728 | tf_op jit(solution)/shard_map/psum | solution.py:284
  333.0 24.9 %all-reduce.1 = (f32[4,1152]{1,0:T(4,128)}, f32[6,768]{1,0:T(8,128)}) all-reduce(f32[4,1152]{1,0:T(4,128)S(1)} %get-tuple-element.122, f32[6,768]{1,0:T(8,128)S(1)} %get-tuple-element.123), channel_id=1, replica_groups=mesh['dp'=8,'mp'=4] {'dp'}, use_global_device_ids=true, to_apply=%region_16.17 | all-reduce | flops 9216 | bytes 73728 | tf_op jit(solution)/shard_map/psum | solution.py:284
  363.4 2.5 fusion.22
  371.7 3.1 fusion.24
  374.8 3.1 fusion.23
  382.1 2.9 gather_fusion.10
  384.9 2.7 gather_fusion.9
  397.6 8.7 %collective-permute-done.36 = bf16[4,2,96,384]{3,2,1,0:T(8,128)(2,1)S(1)} collective-permute-done((bf16[4,2,96,384]{3,2,1,0:T(8,128)(2,1)}, bf16[4,2,96,384]{3,2,1,0:T(8,128)(2,1)S(1)}, u32[]{:S(2)}, u32[]{:S(2)}) %collective-permute-start.36) | collective-permute-done | bytes 589856 | tf_op jit(solution)/shard_map/ppermute | solution.py:89
  407.9 11.1 %collective-permute-done.24 = bf16[4,2,96,384]{3,2,0,1:T(8,128)(2,1)S(1)} collective-permute-done((bf16[4,2,96,384]{3,2,0,1:T(8,128)(2,1)}, bf16[4,2,96,384]{3,2,0,1:T(8,128)(2,1)S(1)}, u32[]{:S(2)}, u32[]{:S(2)}) %collective-permute-start.24) | collective-permute-done | bytes 589856 | tf_op jit(solution)/shard_map/ppermute | solution.py:89
  419.4 4.9 collective-permute-done.49
  427.9 2.8 collective-permute-done.37
  432.4 4.6 collective-permute-done.25
  441.3 4.9 collective-permute-done.38
  448.5 7.2 %collective-permute-done.39 = bf16[96,768]{1,0:T(8,128)(2,1)S(1)} collective-permute-done((bf16[96,768]{1,0:T(8,128)(2,1)S(1)}, bf16[96,768]{1,0:T(8,128)(2,1)S(1)}, u32[]{:S(2)}, u32[]{:S(2)}) %collective-permute-start.39) | collective-permute-done | bytes 147488 | tf_op jit(solution)/shard_map/ppermute | solution.py:86
  462.2 2.9 collective-permute-done.42
  467.5 3.4 collective-permute-done.27
  472.2 3.4 collective-permute-start.30
  482.4 3.4 collective-permute-start.32
  (380 shorter events, 157.4 us)
Async XLA Ops:
  0.7 25.3 %copy-start = (s32[4,512]{1,0:T(4,128)S(1)}, s32[4,512]{1,0:T(4,128)}, u32[]{:S(2)}) copy-start(s32[4,512]{1,0:T(4,128)} %param.31) | copy-start | bytes 24580
  1.7 19.6 %collective-permute-start.16 = (bf16[96,768]{1,0:T(8,128)(2,1)S(1)}, bf16[96,768]{1,0:T(8,128)(2,1)S(1)}, u32[]{:S(2)}, u32[]{:S(2)}) collective-permute-start(bf16[96,768]{1,0:T(8,128)(2,1)S(1)} %constant_dynamic-slice_fusion.1), channel_id=1, source_target_pairs={{0,3},{1,0},{2,1},{3,2},{4,7},{5,4},{6,5},{7,6},{8,11},{9,8},{10,9... | collective-permute-start | bytes 442376 | tf_op jit(solution)/shard_map/ppermute | solution.py:86
  5.9 15.4 %collective-permute-start.15 = (bf16[96,768]{1,0:T(8,128)(2,1)S(1)}, bf16[96,768]{1,0:T(8,128)(2,1)S(1)}, u32[]{:S(2)}, u32[]{:S(2)}) collective-permute-start(bf16[96,768]{1,0:T(8,128)(2,1)S(1)} %constant_dynamic-slice_fusion.1), channel_id=1, source_target_pairs={{0,2},{1,3},{2,0},{3,1},{4,6},{5,7},{6,4},{7,5},{8,10},{9,11},{10,... | collective-permute-start | bytes 442376 | tf_op jit(solution)/shard_map/ppermute | solution.py:86
  5.9 18.7 %collective-permute-start.14 = (bf16[96,768]{1,0:T(8,128)(2,1)S(1)}, bf16[96,768]{1,0:T(8,128)(2,1)S(1)}, u32[]{:S(2)}, u32[]{:S(2)}) collective-permute-start(bf16[96,768]{1,0:T(8,128)(2,1)S(1)} %constant_dynamic-slice_fusion.1), channel_id=1, source_target_pairs={{0,1},{1,2},{2,3},{3,0},{4,5},{5,6},{6,7},{7,4},{8,9},{9,10},{10,1... | collective-permute-start | bytes 442376 | tf_op jit(solution)/shard_map/ppermute | solution.py:86
  7.3 19.3 %collective-permute-start.9 = (bf16[96,768]{1,0:T(8,128)(2,1)S(1)}, bf16[96,768]{1,0:T(8,128)(2,1)S(1)}, u32[]{:S(2)}, u32[]{:S(2)}) collective-permute-start(bf16[96,768]{1,0:T(8,128)(2,1)S(1)} %constant_dynamic-slice_fusion.2), channel_id=1, source_target_pairs={{0,3},{1,0},{2,1},{3,2},{4,7},{5,4},{6,5},{7,6},{8,11},{9,8},{10,9... | collective-permute-start | bytes 442376 | tf_op jit(solution)/shard_map/ppermute | solution.py:86
  10.1 21.2 %collective-permute-start.8 = (bf16[96,768]{1,0:T(8,128)(2,1)S(1)}, bf16[96,768]{1,0:T(8,128)(2,1)S(1)}, u32[]{:S(2)}, u32[]{:S(2)}) collective-permute-start(bf16[96,768]{1,0:T(8,128)(2,1)S(1)} %constant_dynamic-slice_fusion.2), channel_id=1, source_target_pairs={{0,2},{1,3},{2,0},{3,1},{4,6},{5,7},{6,4},{7,5},{8,10},{9,11},{10,... | collective-permute-start | bytes 442376 | tf_op jit(solution)/shard_map/ppermute | solution.py:86
  21.3 11.9 %collective-permute-start.7 = (bf16[96,768]{1,0:T(8,128)(2,1)S(1)}, bf16[96,768]{1,0:T(8,128)(2,1)S(1)}, u32[]{:S(2)}, u32[]{:S(2)}) collective-permute-start(bf16[96,768]{1,0:T(8,128)(2,1)S(1)} %constant_dynamic-slice_fusion.2), channel_id=1, source_target_pairs={{0,1},{1,2},{2,3},{3,0},{4,5},{5,6},{6,7},{7,4},{8,9},{9,10},{10,1... | collective-permute-start | bytes 442376 | tf_op jit(solution)/shard_map/ppermute | solution.py:86
  21.3 13.1 %collective-permute-start.2 = (bf16[104,768]{1,0:T(8,128)(2,1)S(1)}, bf16[104,768]{1,0:T(8,128)(2,1)S(1)}, u32[]{:S(2)}, u32[]{:S(2)}) collective-permute-start(bf16[104,768]{1,0:T(8,128)(2,1)S(1)} %pad_maximum_fusion.19), channel_id=1, source_target_pairs={{0,3},{1,0},{2,1},{3,2},{4,7},{5,4},{6,5},{7,6},{8,11},{9,8},{10,9... | collective-permute-start | bytes 479240 | tf_op jit(solution)/shard_map/ppermute | solution.py:86
  24.6 22.4 %collective-permute-start.18 = (bf16[3,96,768]{2,1,0:T(8,128)(2,1)S(1)}, bf16[3,96,768]{2,1,0:T(8,128)(2,1)S(1)}, u32[]{:S(2)}, u32[]{:S(2)}) collective-permute-start(bf16[3,96,768]{2,1,0:T(8,128)(2,1)S(1)} %get-tuple-element.159), channel_id=1, source_target_pairs={{0,16},{4,20},{8,24},{12,28},{16,0},{20,4},{24,8},{28,12},{1,17},{... | collective-permute-start | bytes 1327112 | tf_op jit(solution)/shard_map/ppermute | solution.py:89
  26.6 18.0 %collective-permute-start.1 = (bf16[104,768]{1,0:T(8,128)(2,1)S(1)}, bf16[104,768]{1,0:T(8,128)(2,1)S(1)}, u32[]{:S(2)}, u32[]{:S(2)}) collective-permute-start(bf16[104,768]{1,0:T(8,128)(2,1)S(1)} %pad_maximum_fusion.19), channel_id=1, source_target_pairs={{0,2},{1,3},{2,0},{3,1},{4,6},{5,7},{6,4},{7,5},{8,10},{9,11},{10,... | collective-permute-start | bytes 479240 | tf_op jit(solution)/shard_map/ppermute | solution.py:86
  31.3 14.5 %collective-permute-start = (bf16[104,768]{1,0:T(8,128)(2,1)S(1)}, bf16[104,768]{1,0:T(8,128)(2,1)S(1)}, u32[]{:S(2)}, u32[]{:S(2)}) collective-permute-start(bf16[104,768]{1,0:T(8,128)(2,1)S(1)} %pad_maximum_fusion.19), channel_id=1, source_target_pairs={{0,1},{1,2},{2,3},{3,0},{4,5},{5,6},{6,7},{7,4},{8,9},{9,10},{10,1... | collective-permute-start | bytes 479240 | tf_op jit(solution)/shard_map/ppermute | solution.py:86
  33.1 14.2 %collective-permute-start.17 = (bf16[3,96,768]{2,1,0:T(8,128)(2,1)S(1)}, bf16[3,96,768]{2,1,0:T(8,128)(2,1)S(1)}, u32[]{:S(2)}, u32[]{:S(2)}) collective-permute-start(bf16[3,96,768]{2,1,0:T(8,128)(2,1)S(1)} %get-tuple-element.159), channel_id=1, source_target_pairs={{0,8},{4,12},{8,0},{12,4},{16,24},{20,28},{24,16},{28,20},{1,9},{5... | collective-permute-start | bytes 1327112 | tf_op jit(solution)/shard_map/ppermute | solution.py:89
  34.4 16.2 %collective-permute-start.19 = (bf16[3,96,768]{2,1,0:T(8,128)(2,1)S(1)}, bf16[3,96,768]{2,1,0:T(8,128)(2,1)S(1)}, u32[]{:S(2)}, u32[]{:S(2)}) collective-permute-start(bf16[3,96,768]{2,1,0:T(8,128)(2,1)S(1)} %get-tuple-element.159), channel_id=1, source_target_pairs={{0,24},{4,28},{8,16},{12,20},{16,8},{20,12},{24,0},{28,4},{1,25},{... | collective-permute-start | bytes 1327112 | tf_op jit(solution)/shard_map/ppermute | solution.py:89
  44.6 20.0 %collective-permute-start.11 = (bf16[3,96,768]{2,1,0:T(8,128)(2,1)S(1)}, bf16[3,96,768]{2,1,0:T(8,128)(2,1)S(1)}, u32[]{:S(2)}, u32[]{:S(2)}) collective-permute-start(bf16[3,96,768]{2,1,0:T(8,128)(2,1)S(1)} %get-tuple-element.163), channel_id=1, source_target_pairs={{0,16},{4,20},{8,24},{12,28},{16,0},{20,4},{24,8},{28,12},{1,17},{... | collective-permute-start | bytes 1327112 | tf_op jit(solution)/shard_map/ppermute | solution.py:89
  45.8 18.7 %collective-permute-start.10 = (bf16[3,96,768]{2,1,0:T(8,128)(2,1)S(1)}, bf16[3,96,768]{2,1,0:T(8,128)(2,1)S(1)}, u32[]{:S(2)}, u32[]{:S(2)}) collective-permute-start(bf16[3,96,768]{2,1,0:T(8,128)(2,1)S(1)} %get-tuple-element.163), channel_id=1, source_target_pairs={{0,8},{4,12},{8,0},{12,4},{16,24},{20,28},{24,16},{28,20},{1,9},{5... | collective-permute-start | bytes 1327112 | tf_op jit(solution)/shard_map/ppermute | solution.py:89
  47.0 22.6 %collective-permute-start.12 = (bf16[3,96,768]{2,1,0:T(8,128)(2,1)S(1)}, bf16[3,96,768]{2,1,0:T(8,128)(2,1)S(1)}, u32[]{:S(2)}, u32[]{:S(2)}) collective-permute-start(bf16[3,96,768]{2,1,0:T(8,128)(2,1)S(1)} %get-tuple-element.163), channel_id=1, source_target_pairs={{0,24},{4,28},{8,16},{12,20},{16,8},{20,12},{24,0},{28,4},{1,25},{... | collective-permute-start | bytes 1327112 | tf_op jit(solution)/shard_map/ppermute | solution.py:89
  52.7 53.2 %collective-permute-start.20 = (bf16[4,3,96,768]{3,2,1,0:T(8,128)(2,1)}, bf16[4,3,96,768]{3,2,1,0:T(8,128)(2,1)S(1)}, u32[]{:S(2)}, u32[]{:S(2)}) collective-permute-start(bf16[4,3,96,768]{3,2,1,0:T(8,128)(2,1)} %get-tuple-element.137), channel_id=1, source_target_pairs={{0,4},{4,0},{8,12},{12,8},{16,20},{20,16},{24,28},{28,24},{1,5},{5... | collective-permute-start | bytes 5308424 | tf_op jit(solution)/shard_map/ppermute | solution.py:89
  71.7 44.5 %collective-permute-start.13 = (bf16[4,3,96,768]{3,2,1,0:T(8,128)(2,1)}, bf16[4,3,96,768]{3,2,1,0:T(8,128)(2,1)}, u32[]{:S(2)}, u32[]{:S(2)}) collective-permute-start(bf16[4,3,96,768]{3,2,1,0:T(8,128)(2,1)} %get-tuple-element.141), channel_id=1, source_target_pairs={{0,4},{4,0},{8,12},{12,8},{16,20},{20,16},{24,28},{28,24},{1,5},{5... | collective-permute-start | bytes 5308424 | tf_op jit(solution)/shard_map/ppermute | solution.py:89
  77.2 11.9 %collective-permute-start.4 = (bf16[3,96,768]{2,1,0:T(8,128)(2,1)S(1)}, bf16[3,96,768]{2,1,0:T(8,128)(2,1)S(1)}, u32[]{:S(2)}, u32[]{:S(2)}) collective-permute-start(bf16[3,96,768]{2,1,0:T(8,128)(2,1)S(1)} %get-tuple-element.161), channel_id=1, source_target_pairs={{0,16},{4,20},{8,24},{12,28},{16,0},{20,4},{24,8},{28,12},{1,17},{... | collective-permute-start | bytes 1327112 | tf_op jit(solution)/shard_map/ppermute | solution.py:89
  77.5 11.6 %collective-permute-start.3 = (bf16[3,96,768]{2,1,0:T(8,128)(2,1)S(1)}, bf16[3,96,768]{2,1,0:T(8,128)(2,1)S(1)}, u32[]{:S(2)}, u32[]{:S(2)}) collective-permute-start(bf16[3,96,768]{2,1,0:T(8,128)(2,1)S(1)} %get-tuple-element.161), channel_id=1, source_target_pairs={{0,8},{4,12},{8,0},{12,4},{16,24},{20,28},{24,16},{28,20},{1,9},{5... | collective-permute-start | bytes 1327112 | tf_op jit(solution)/shard_map/ppermute | solution.py:89
  78.7 20.7 %collective-permute-start.5 = (bf16[3,96,768]{2,1,0:T(8,128)(2,1)S(1)}, bf16[3,96,768]{2,1,0:T(8,128)(2,1)S(1)}, u32[]{:S(2)}, u32[]{:S(2)}) collective-permute-start(bf16[3,96,768]{2,1,0:T(8,128)(2,1)S(1)} %get-tuple-element.161), channel_id=1, source_target_pairs={{0,24},{4,28},{8,16},{12,20},{16,8},{20,12},{24,0},{28,4},{1,25},{... | collective-permute-start | bytes 1327112 | tf_op jit(solution)/shard_map/ppermute | solution.py:89
  101.5 35.3 %collective-permute-start.6 = (bf16[4,3,96,768]{3,2,1,0:T(8,128)(2,1)}, bf16[4,3,96,768]{3,2,1,0:T(8,128)(2,1)}, u32[]{:S(2)}, u32[]{:S(2)}) collective-permute-start(bf16[4,3,96,768]{3,2,1,0:T(8,128)(2,1)} %get-tuple-element.139), channel_id=1, source_target_pairs={{0,4},{4,0},{8,12},{12,8},{16,20},{20,16},{24,28},{28,24},{1,5},{5... | collective-permute-start | bytes 5308424 | tf_op jit(solution)/shard_map/ppermute | solution.py:89
  103.8 35.1 %copy-start.34 = (s32[1024]{0:T(1024)}, s32[1024]{0:T(1024)S(1)}, u32[]{:S(2)}) copy-start(s32[1024]{0:T(1024)S(1)} %pad_clamp_fusion.3) | copy-start | bytes 12292
  212.8 17.0 %slice-start = ((s8[12582912]{0:T(1024)(128)(4,1)}), s8[4194304]{0:T(1024)(128)(4,1)S(1)}, s32[]{:S(2)}) async-start(s8[12582912]{0:T(1024)(128)(4,1)} %bitcast.346), calls=%async_computation | async-start | bytes 8388608
  212.8 17.0 %slice-start.1 = ((s8[12582912]{0:T(1024)(128)(4,1)}), s8[4194304]{0:T(1024)(128)(4,1)S(1)}, s32[]{:S(2)}) async-start(s8[12582912]{0:T(1024)(128)(4,1)} %bitcast.346), calls=%async_computation.1 | async-start | bytes 8388608
  260.6 102.8 %collective-permute-start.45 = (bf16[4,4,96,768]{3,2,1,0:T(8,128)(2,1)}, bf16[4,4,96,768]{3,2,1,0:T(8,128)(2,1)}, u32[]{:S(2)}, u32[]{:S(2)}) collective-permute-start(bf16[4,4,96,768]{3,2,1,0:T(8,128)(2,1)} %slice_bitcast_fusion), channel_id=1, source_target_pairs={{0,4},{4,0},{8,12},{12,8},{16,20},{20,16},{24,28},{28,24},{1,5},{5... | collective-permute-start | bytes 7077896 | tf_op jit(solution)/shard_map/ppermute | solution.py:89
  311.5 60.3 %collective-permute-start.21 = (bf16[4,4,96,768]{3,2,0,1:T(8,128)(2,1)}, bf16[4,4,96,768]{3,2,0,1:T(8,128)(2,1)}, u32[]{:S(2)}, u32[]{:S(2)}) collective-permute-start(bf16[4,4,96,768]{3,2,0,1:T(8,128)(2,1)} %slice_bitcast_fusion.2), channel_id=1, source_target_pairs={{0,4},{4,0},{8,12},{12,8},{16,20},{20,16},{24,28},{28,24},{1,5},{5... | collective-permute-start | bytes 7077896 | tf_op jit(solution)/shard_map/ppermute | solution.py:89
  311.6 46.3 %copy-start.17 = (bf16[12,64,512]{2,1,0:T(8,128)(2,1)S(1)}, bf16[12,64,512]{2,1,0:T(8,128)(2,1)}, u32[]{:S(2)}) copy-start(bf16[12,64,512]{2,1,0:T(8,128)(2,1)} %get-tuple-element.180) | copy-start | bytes 2359300
  311.6 48.5 %copy-start.32 = (bf16[12,64,512]{2,1,0:T(8,128)(2,1)S(1)}, bf16[12,64,512]{2,1,0:T(8,128)(2,1)}, u32[]{:S(2)}) copy-start(bf16[12,64,512]{2,1,0:T(8,128)(2,1)} %multiply_convert_fusion.1) | copy-start | bytes 2359300
  313.2 61.7 %collective-permute-start.33 = (bf16[4,4,96,768]{3,2,1,0:T(8,128)(2,1)}, bf16[4,4,96,768]{3,2,1,0:T(8,128)(2,1)}, u32[]{:S(2)}, u32[]{:S(2)}) collective-permute-start(bf16[4,4,96,768]{3,2,1,0:T(8,128)(2,1)} %slice_bitcast_fusion.1), channel_id=1, source_target_pairs={{0,4},{4,0},{8,12},{12,8},{16,20},{20,16},{24,28},{28,24},{1,5},{5... | collective-permute-start | bytes 7077896 | tf_op jit(solution)/shard_map/ppermute | solution.py:89
  367.6 25.7 %collective-permute-start.48 = (bf16[4,2,96,384]{3,2,1,0:T(8,128)(2,1)}, bf16[4,2,96,384]{3,2,1,0:T(8,128)(2,1)}, u32[]{:S(2)}, u32[]{:S(2)}) collective-permute-start(bf16[4,2,96,384]{3,2,1,0:T(8,128)(2,1)} %slice.423), channel_id=1, source_target_pairs={{0,16},{4,20},{8,24},{12,28},{16,0},{20,4},{24,8},{28,12},{1,17},{... | collective-permute-start | bytes 1769480 | tf_op jit(solution)/shard_map/ppermute | solution.py:89
  369.4 26.8 %collective-permute-start.46 = (bf16[4,2,96,384]{3,2,0,1:T(8,128)(2,1)}, bf16[4,2,96,384]{3,2,0,1:T(8,128)(2,1)}, u32[]{:S(2)}, u32[]{:S(2)}) collective-permute-start(bf16[4,2,96,384]{3,2,0,1:T(8,128)(2,1)} %bitcast.161), channel_id=1, source_target_pairs={{0,8},{4,12},{8,0},{12,4},{16,24},{20,28},{24,16},{28,20},{1,9},{5... | collective-permute-start | bytes 1769480 | tf_op jit(solution)/shard_map/ppermute | solution.py:89
  391.8 14.5 %collective-permute-start.36 = (bf16[4,2,96,384]{3,2,1,0:T(8,128)(2,1)}, bf16[4,2,96,384]{3,2,1,0:T(8,128)(2,1)S(1)}, u32[]{:S(2)}, u32[]{:S(2)}) collective-permute-start(bf16[4,2,96,384]{3,2,1,0:T(8,128)(2,1)} %slice.408), channel_id=1, source_target_pairs={{0,16},{4,20},{8,24},{12,28},{16,0},{20,4},{24,8},{28,12},{1,17},{... | collective-permute-start | bytes 1769480 | tf_op jit(solution)/shard_map/ppermute | solution.py:89
  392.1 15.5 %collective-permute-start.34 = (bf16[4,2,96,384]{3,2,0,1:T(8,128)(2,1)}, bf16[4,2,96,384]{3,2,0,1:T(8,128)(2,1)S(1)}, u32[]{:S(2)}, u32[]{:S(2)}) collective-permute-start(bf16[4,2,96,384]{3,2,0,1:T(8,128)(2,1)} %bitcast.421), channel_id=1, source_target_pairs={{0,8},{4,12},{8,0},{12,4},{16,24},{20,28},{24,16},{28,20},{1,9},{5... | collective-permute-start | bytes 1769480 | tf_op jit(solution)/shard_map/ppermute | solution.py:89
  392.2 26.7 %collective-permute-start.24 = (bf16[4,2,96,384]{3,2,0,1:T(8,128)(2,1)}, bf16[4,2,96,384]{3,2,0,1:T(8,128)(2,1)S(1)}, u32[]{:S(2)}, u32[]{:S(2)}) collective-permute-start(bf16[4,2,96,384]{3,2,0,1:T(8,128)(2,1)} %slice.386), channel_id=1, source_target_pairs={{0,16},{4,20},{8,24},{12,28},{16,0},{20,4},{24,8},{28,12},{1,17},{... | collective-permute-start | bytes 1769480 | tf_op jit(solution)/shard_map/ppermute | solution.py:89
  393.3 25.9 %collective-permute-start.22 = (bf16[4,2,96,384]{3,2,0,1:T(8,128)(2,1)}, bf16[4,2,96,384]{3,2,0,1:T(8,128)(2,1)S(1)}, u32[]{:S(2)}, u32[]{:S(2)}) collective-permute-start(bf16[4,2,96,384]{3,2,0,1:T(8,128)(2,1)} %bitcast.420), channel_id=1, source_target_pairs={{0,8},{4,12},{8,0},{12,4},{16,24},{20,28},{24,16},{28,20},{1,9},{5... | collective-permute-start | bytes 1769480 | tf_op jit(solution)/shard_map/ppermute | solution.py:89
  396.2 28.1 %collective-permute-start.49 = (bf16[4,96,384]{2,1,0:T(8,128)(2,1)S(1)}, bf16[4,96,384]{2,1,0:T(8,128)(2,1)S(1)}, u32[]{:S(2)}, u32[]{:S(2)}) collective-permute-start(bf16[4,96,384]{2,1,0:T(8,128)(2,1)S(1)} %slice_bitcast_fusion.5), channel_id=1, source_target_pairs={{0,8},{4,12},{8,0},{12,4},{16,24},{20,28},{24,16},{28,20},{1,9},{5... | collective-permute-start | bytes 884744 | tf_op jit(solution)/shard_map/ppermute | solution.py:89
  406.3 20.2 %collective-permute-start.47 = (bf16[4,96,384]{2,1,0:T(8,128)(2,1)S(1)}, bf16[4,96,384]{2,1,0:T(8,128)(2,1)S(1)}, u32[]{:S(2)}, u32[]{:S(2)}) collective-permute-start(bf16[4,96,384]{2,1,0:T(8,128)(2,1)S(1)} %slice_bitcast_fusion.7), channel_id=1, source_target_pairs={{0,16},{4,20},{8,24},{12,28},{16,0},{20,4},{24,8},{28,12},{1,17},{... | collective-permute-start | bytes 884744 | tf_op jit(solution)/shard_map/ppermute | solution.py:89
  407.6 23.1 %collective-permute-start.37 = (bf16[4,96,384]{2,1,0:T(8,128)(2,1)S(1)}, bf16[4,96,384]{2,1,0:T(8,128)(2,1)S(1)}, u32[]{:S(2)}, u32[]{:S(2)}) collective-permute-start(bf16[4,96,384]{2,1,0:T(8,128)(2,1)S(1)} %slice_bitcast_fusion.9), channel_id=1, source_target_pairs={{0,8},{4,12},{8,0},{12,4},{16,24},{20,28},{24,16},{28,20},{1,9},{5... | collective-permute-start | bytes 884744 | tf_op jit(solution)/shard_map/ppermute | solution.py:89
  419.0 12.6 %collective-permute-start.35 = (bf16[4,96,384]{2,1,0:T(8,128)(2,1)S(1)}, bf16[4,96,384]{2,1,0:T(8,128)(2,1)S(1)}, u32[]{:S(2)}, u32[]{:S(2)}) collective-permute-start(bf16[4,96,384]{2,1,0:T(8,128)(2,1)S(1)} %slice_bitcast_fusion.11), channel_id=1, source_target_pairs={{0,16},{4,20},{8,24},{12,28},{16,0},{20,4},{24,8},{28,12},{1,17},{... | collective-permute-start | bytes 884744 | tf_op jit(solution)/shard_map/ppermute | solution.py:89
  419.2 17.8 %collective-permute-start.25 = (bf16[4,96,384]{2,1,0:T(8,128)(2,1)S(1)}, bf16[4,96,384]{2,1,0:T(8,128)(2,1)S(1)}, u32[]{:S(2)}, u32[]{:S(2)}) collective-permute-start(bf16[4,96,384]{2,1,0:T(8,128)(2,1)S(1)} %slice_bitcast_fusion.13), channel_id=1, source_target_pairs={{0,8},{4,12},{8,0},{12,4},{16,24},{20,28},{24,16},{28,20},{1,9},{5... | collective-permute-start | bytes 884744 | tf_op jit(solution)/shard_map/ppermute | solution.py:89
  424.4 32.2 %collective-permute-start.23 = (bf16[4,96,384]{2,1,0:T(8,128)(2,1)S(1)}, bf16[4,96,384]{2,1,0:T(8,128)(2,1)S(1)}, u32[]{:S(2)}, u32[]{:S(2)}) collective-permute-start(bf16[4,96,384]{2,1,0:T(8,128)(2,1)S(1)} %slice_bitcast_fusion.15), channel_id=1, source_target_pairs={{0,16},{4,20},{8,24},{12,28},{16,0},{20,4},{24,8},{28,12},{1,17},{... | collective-permute-start | bytes 884744 | tf_op jit(solution)/shard_map/ppermute | solution.py:89
  426.6 11.6 %collective-permute-start.50 = (bf16[96,768]{1,0:T(8,128)(2,1)S(1)}, bf16[96,768]{1,0:T(8,128)(2,1)S(1)}, u32[]{:S(2)}, u32[]{:S(2)}) collective-permute-start(bf16[96,768]{1,0:T(8,128)(2,1)S(1)} %get-tuple-element.145), channel_id=1, source_target_pairs={{0,3},{1,0},{2,1},{3,2},{4,7},{5,4},{6,5},{7,6},{8,11},{9,8},{10,9... | collective-permute-start | bytes 442376 | tf_op jit(solution)/shard_map/ppermute | solution.py:86
  430.7 7.9 %collective-permute-start.52 = (bf16[96,768]{1,0:T(8,128)(2,1)S(1)}, bf16[96,768]{1,0:T(8,128)(2,1)S(1)}, u32[]{:S(2)}, u32[]{:S(2)}) collective-permute-start(bf16[96,768]{1,0:T(8,128)(2,1)S(1)} %get-tuple-element.146), channel_id=1, source_target_pairs={{0,1},{1,2},{2,3},{3,0},{4,5},{5,6},{6,7},{7,4},{8,9},{9,10},{10,1... | collective-permute-start | bytes 442376 | tf_op jit(solution)/shard_map/ppermute | solution.py:86
  431.6 8.3 %collective-permute-start.51 = (bf16[96,768]{1,0:T(8,128)(2,1)S(1)}, bf16[96,768]{1,0:T(8,128)(2,1)S(1)}, u32[]{:S(2)}, u32[]{:S(2)}) collective-permute-start(bf16[96,768]{1,0:T(8,128)(2,1)S(1)} %get-tuple-element.147), channel_id=1, source_target_pairs={{0,2},{1,3},{2,0},{3,1},{4,6},{5,7},{6,4},{7,5},{8,10},{9,11},{10,... | collective-permute-start | bytes 442376 | tf_op jit(solution)/shard_map/ppermute | solution.py:86
  437.0 9.2 %collective-permute-start.38 = (bf16[96,768]{1,0:T(8,128)(2,1)S(1)}, bf16[96,768]{1,0:T(8,128)(2,1)S(1)}, u32[]{:S(2)}, u32[]{:S(2)}) collective-permute-start(bf16[96,768]{1,0:T(8,128)(2,1)S(1)} %get-tuple-element.150), channel_id=1, source_target_pairs={{0,3},{1,0},{2,1},{3,2},{4,7},{5,4},{6,5},{7,6},{8,11},{9,8},{10,9... | collective-permute-start | bytes 442376 | tf_op jit(solution)/shard_map/ppermute | solution.py:86
  438.2 10.3 %collective-permute-start.40 = (bf16[96,768]{1,0:T(8,128)(2,1)S(1)}, bf16[96,768]{1,0:T(8,128)(2,1)S(1)}, u32[]{:S(2)}, u32[]{:S(2)}) collective-permute-start(bf16[96,768]{1,0:T(8,128)(2,1)S(1)} %get-tuple-element.151), channel_id=1, source_target_pairs={{0,1},{1,2},{2,3},{3,0},{4,5},{5,6},{6,7},{7,4},{8,9},{9,10},{10,1... | collective-permute-start | bytes 442376 | tf_op jit(solution)/shard_map/ppermute | solution.py:86
  438.6 17.1 %collective-permute-start.39 = (bf16[96,768]{1,0:T(8,128)(2,1)S(1)}, bf16[96,768]{1,0:T(8,128)(2,1)S(1)}, u32[]{:S(2)}, u32[]{:S(2)}) collective-permute-start(bf16[96,768]{1,0:T(8,128)(2,1)S(1)} %get-tuple-element.152), channel_id=1, source_target_pairs={{0,2},{1,3},{2,0},{3,1},{4,6},{5,7},{6,4},{7,5},{8,10},{9,11},{10,... | collective-permute-start | bytes 442376 | tf_op jit(solution)/shard_map/ppermute | solution.py:86
  440.0 18.0 %collective-permute-start.55 = (bf16[96,768]{1,0:T(8,128)(2,1)S(1)}, bf16[96,768]{1,0:T(8,128)(2,1)S(1)}, u32[]{:S(2)}, u32[]{:S(2)}) collective-permute-start(bf16[96,768]{1,0:T(8,128)(2,1)S(1)} %fusion.58), channel_id=1, source_target_pairs={{0,24},{4,28},{8,16},{12,20},{16,8},{20,12},{24,0},{28,4},{1,25},{... | collective-permute-start | bytes 442376 | tf_op jit(solution)/shard_map/ppermute | solution.py:89
  446.2 13.2 %collective-permute-start.54 = (bf16[96,768]{1,0:T(8,128)(2,1)S(1)}, bf16[96,768]{1,0:T(8,128)(2,1)S(1)}, u32[]{:S(2)}, u32[]{:S(2)}) collective-permute-start(bf16[96,768]{1,0:T(8,128)(2,1)S(1)} %fusion.58), channel_id=1, source_target_pairs={{0,16},{4,20},{8,24},{12,28},{16,0},{20,4},{24,8},{28,12},{1,17},{... | collective-permute-start | bytes 442376 | tf_op jit(solution)/shard_map/ppermute | solution.py:89
  448.5 11.7 %collective-permute-start.53 = (bf16[96,768]{1,0:T(8,128)(2,1)S(1)}, bf16[96,768]{1,0:T(8,128)(2,1)S(1)}, u32[]{:S(2)}, u32[]{:S(2)}) collective-permute-start(bf16[96,768]{1,0:T(8,128)(2,1)S(1)} %fusion.58), channel_id=1, source_target_pairs={{0,8},{4,12},{8,0},{12,4},{16,24},{20,28},{24,16},{28,20},{1,9},{5... | collective-permute-start | bytes 442376 | tf_op jit(solution)/shard_map/ppermute | solution.py:89
  455.8 6.3 %collective-permute-start.43 = (bf16[96,768]{1,0:T(8,128)(2,1)S(1)}, bf16[96,768]{1,0:T(8,128)(2,1)S(1)}, u32[]{:S(2)}, u32[]{:S(2)}) collective-permute-start(bf16[96,768]{1,0:T(8,128)(2,1)S(1)} %fusion.61), channel_id=1, source_target_pairs={{0,24},{4,28},{8,16},{12,20},{16,8},{20,12},{24,0},{28,4},{1,25},{... | collective-permute-start | bytes 442376 | tf_op jit(solution)/shard_map/ppermute | solution.py:89
  456.7 8.5 %collective-permute-start.42 = (bf16[96,768]{1,0:T(8,128)(2,1)S(1)}, bf16[96,768]{1,0:T(8,128)(2,1)S(1)}, u32[]{:S(2)}, u32[]{:S(2)}) collective-permute-start(bf16[96,768]{1,0:T(8,128)(2,1)S(1)} %fusion.61), channel_id=1, source_target_pairs={{0,16},{4,20},{8,24},{12,28},{16,0},{20,4},{24,8},{28,12},{1,17},{... | collective-permute-start | bytes 442376 | tf_op jit(solution)/shard_map/ppermute | solution.py:89
  458.0 9.3 %collective-permute-start.41 = (bf16[96,768]{1,0:T(8,128)(2,1)S(1)}, bf16[96,768]{1,0:T(8,128)(2,1)S(1)}, u32[]{:S(2)}, u32[]{:S(2)}) collective-permute-start(bf16[96,768]{1,0:T(8,128)(2,1)S(1)} %fusion.61), channel_id=1, source_target_pairs={{0,8},{4,12},{8,0},{12,4},{16,24},{20,28},{24,16},{28,20},{1,9},{5... | collective-permute-start | bytes 442376 | tf_op jit(solution)/shard_map/ppermute | solution.py:89
  459.3 8.2 %collective-permute-start.26 = (bf16[96,768]{1,0:T(8,128)(2,1)S(1)}, bf16[96,768]{1,0:T(8,128)(2,1)S(1)}, u32[]{:S(2)}, u32[]{:S(2)}) collective-permute-start(bf16[96,768]{1,0:T(8,128)(2,1)S(1)} %get-tuple-element.155), channel_id=1, source_target_pairs={{0,3},{1,0},{2,1},{3,2},{4,7},{5,4},{6,5},{7,6},{8,11},{9,8},{10,9... | collective-permute-start | bytes 442376 | tf_op jit(solution)/shard_map/ppermute | solution.py:86
  460.2 7.3 %collective-permute-start.28 = (bf16[96,768]{1,0:T(8,128)(2,1)S(1)}, bf16[96,768]{1,0:T(8,128)(2,1)S(1)}, u32[]{:S(2)}, u32[]{:S(2)}) collective-permute-start(bf16[96,768]{1,0:T(8,128)(2,1)S(1)} %get-tuple-element.156), channel_id=1, source_target_pairs={{0,1},{1,2},{2,3},{3,0},{4,5},{5,6},{6,7},{7,4},{8,9},{9,10},{10,1... | collective-permute-start | bytes 442376 | tf_op jit(solution)/shard_map/ppermute | solution.py:86
  462.1 8.8 %collective-permute-start.27 = (bf16[96,768]{1,0:T(8,128)(2,1)S(1)}, bf16[96,768]{1,0:T(8,128)(2,1)S(1)}, u32[]{:S(2)}, u32[]{:S(2)}) collective-permute-start(bf16[96,768]{1,0:T(8,128)(2,1)S(1)} %get-tuple-element.157), channel_id=1, source_target_pairs={{0,2},{1,3},{2,0},{3,1},{4,6},{5,7},{6,4},{7,5},{8,10},{9,11},{10,... | collective-permute-start | bytes 442376 | tf_op jit(solution)/shard_map/ppermute | solution.py:86
  462.1 17.4 %copy-start.36 = (f32[6,768]{1,0:T(8,128)S(1)}, f32[6,768]{1,0:T(8,128)}, u32[]{:S(2)}) copy-start(f32[6,768]{1,0:T(8,128)} %get-tuple-element.121) | copy-start | bytes 55300
  465.1 20.7 %collective-permute-start.56 = (bf16[4,96,768]{2,1,0:T(8,128)(2,1)S(1)}, bf16[4,96,768]{2,1,0:T(8,128)(2,1)S(1)}, u32[]{:S(2)}, u32[]{:S(2)}) collective-permute-start(bf16[4,96,768]{2,1,0:T(8,128)(2,1)S(1)} %get-tuple-element.144), channel_id=1, source_target_pairs={{0,4},{4,0},{8,12},{12,8},{16,20},{20,16},{24,28},{28,24},{1,5},{5... | collective-permute-start | bytes 1769480 | tf_op jit(solution)/shard_map/ppermute | solution.py:89
  467.4 19.2 %collective-permute-start.44 = (bf16[4,96,768]{2,1,0:T(8,128)(2,1)S(1)}, bf16[4,96,768]{2,1,0:T(8,128)(2,1)}, u32[]{:S(2)}, u32[]{:S(2)}) collective-permute-start(bf16[4,96,768]{2,1,0:T(8,128)(2,1)S(1)} %get-tuple-element.149), channel_id=1, source_target_pairs={{0,4},{4,0},{8,12},{12,8},{16,20},{20,16},{24,28},{28,24},{1,5},{5... | collective-permute-start | bytes 1769480 | tf_op jit(solution)/shard_map/ppermute | solution.py:89
  471.0 9.1 %collective-permute-start.31 = (bf16[96,768]{1,0:T(8,128)(2,1)S(1)}, bf16[96,768]{1,0:T(8,128)(2,1)S(1)}, u32[]{:S(2)}, u32[]{:S(2)}) collective-permute-start(bf16[96,768]{1,0:T(8,128)(2,1)S(1)} %fusion.64), channel_id=1, source_target_pairs={{0,24},{4,28},{8,16},{12,20},{16,8},{20,12},{24,0},{28,4},{1,25},{... | collective-permute-start | bytes 442376 | tf_op jit(solution)/shard_map/ppermute | solution.py:89
  472.2 7.9 %collective-permute-start.30 = (bf16[96,768]{1,0:T(8,128)(2,1)S(1)}, bf16[96,768]{1,0:T(8,128)(2,1)S(1)}, u32[]{:S(2)}, u32[]{:S(2)}) collective-permute-start(bf16[96,768]{1,0:T(8,128)(2,1)S(1)} %fusion.64), channel_id=1, source_target_pairs={{0,16},{4,20},{8,24},{12,28},{16,0},{20,4},{24,8},{28,12},{1,17},{... | collective-permute-start | bytes 442376 | tf_op jit(solution)/shard_map/ppermute | solution.py:89
  475.6 5.7 %collective-permute-start.29 = (bf16[96,768]{1,0:T(8,128)(2,1)S(1)}, bf16[96,768]{1,0:T(8,128)(2,1)S(1)}, u32[]{:S(2)}, u32[]{:S(2)}) collective-permute-start(bf16[96,768]{1,0:T(8,128)(2,1)S(1)} %fusion.64), channel_id=1, source_target_pairs={{0,8},{4,12},{8,0},{12,4},{16,24},{20,28},{24,16},{28,20},{1,9},{5... | collective-permute-start | bytes 442376 | tf_op jit(solution)/shard_map/ppermute | solution.py:89
  482.4 9.5 %collective-permute-start.32 = (bf16[4,96,768]{2,1,0:T(8,128)(2,1)}, bf16[4,96,768]{2,1,0:T(8,128)(2,1)}, u32[]{:S(2)}, u32[]{:S(2)}) collective-permute-start(bf16[4,96,768]{2,1,0:T(8,128)(2,1)} %get-tuple-element.154), channel_id=1, source_target_pairs={{0,4},{4,0},{8,12},{12,8},{16,20},{20,16},{24,28},{28,24},{1,5},{5... | collective-permute-start | bytes 1769480 | tf_op jit(solution)/shard_map/ppermute | solution.py:89
  (56 other events, 269.3 us)
